TPU v7x, 32 devices: a whole 2x2x4 slice. The times are simulated.
32 devices in a mesh: ctx: 4 (over y, core), fsdp: 8 (over z, x).
Axes of the slice: x: 2, y: 2, z: 4, core: 2. Of those that a mesh axis runs over, the one named last changes fastest.
Arguments:
- tokens: bfloat16 [8, 1024, 512], P('fsdp', 'ctx'), may hold values from -6 to 6
- segment_ids: int32 [8, 1024], P('fsdp'), may hold values from 0 to 3, never falling along the last dimension, each value on 1 to 384 neighbouring positions
- bucket_table: int32 [1024], replicated, may hold values from 0 to 31
- w_qkv: bfloat16 [512, 1536], P('fsdp'), may hold values from -0.25 to 0.25
- w_out: bfloat16 [512, 512], P('fsdp'), may hold values from -2 to 2
- w_in: bfloat16 [512, 2048], P('fsdp'), may hold values from -0.25 to 0.25
- w_down: bfloat16 [2048, 512], P('fsdp'), may hold values from -0.125 to 0.125
- gain_one: bfloat16 [512], P('fsdp'), may hold values from 0.5 to 1.5
- shift_one: bfloat16 [512], P('fsdp'), may hold values from -1.75 to 1.75
- gain_two: bfloat16 [512], P('fsdp'), may hold values from 0.5 to 1.5
- shift_two: bfloat16 [512], P('fsdp'), may hold values from -1.75 to 1.75
- bias_in: bfloat16 [2048], P('fsdp'), may hold values from -1.75 to 1.75
- bias_down: bfloat16 [512], P('fsdp'), may hold values from -1.75 to 1.75
- rel_bias: bfloat16 [32, 8], replicated, may hold values from -6 to 6
- cotangent: bfloat16 [8, 1024, 512], P('fsdp', 'ctx'), may hold values from -6 to 6
Outputs:
- output: bfloat16 [8, 1024, 512], P('fsdp', 'ctx')
- input_grad: bfloat16 [8, 1024, 512], P('fsdp', 'ctx')
- grad_qkv: float32 [512, 1536], P('fsdp')
- grad_out: float32 [512, 512], P('fsdp')
- grad_in: float32 [512, 2048], P('fsdp')
- grad_down: float32 [2048, 512], P('fsdp')
- grad_gain_one: float32 [512], P('fsdp')
- grad_shift_one: float32 [512], P('fsdp')
- grad_gain_two: float32 [512], P('fsdp')
- grad_shift_two: float32 [512], P('fsdp')
- grad_bias_in: float32 [2048], P('fsdp')
- grad_bias_down: float32 [512], P('fsdp')
- grad_rel_bias: float32 [32, 8], replicated
Inputs may be any that keep to these rules, and one draw needn't show every extreme that they name: `segment_ids`: along each group the segment number never falls; segment 0 is the group's prompt and segment k > 0 its k-th continuation; each segment has 1 to 384 tokens, one exactly 384.
All inputs are finite; a program needn't handle non-finite values.
Results may differ from a plain program's by a relative error of at most 0.024.
Values may be sent and summed in bfloat16 or wider, within the bound.
A program may use at most 128 MiB of HBM per device.

v0:
```python
import jax
import jax.numpy as jnp
from jax import lax
from jax.sharding import PartitionSpec as P

norm_eps = 1e-05
masked_low = -1e30


def norm_layer(features, gain_vec, shift_vec):
    centre = jnp.mean(features, axis=-1, keepdims=True)
    centred = features - centre
    spread = jnp.mean(centred * centred, axis=-1, keepdims=True)
    return centred * lax.rsqrt(spread + norm_eps) * gain_vec + shift_vec


def exact_gelu(features):
    return jax.nn.gelu(features, approximate=False)


def allowed_block(query_pos, query_seg, key_pos, key_seg):
    causal = key_pos[None, :] <= query_pos[:, None]
    shared = (key_seg[None, :] == 0) | (key_seg[None, :] == query_seg[:, None])
    return causal & shared


def bias_band(query_first, key_first, size_rows, size_cols, bucket_table, bias_heads):
    span = size_rows + size_cols - 1
    offsets = jnp.arange(span, dtype=jnp.int32) - (size_cols - 1) + query_first - key_first
    per_distance = bias_heads[:, bucket_table[jnp.clip(offsets, 0, bucket_table.shape[0] - 1)]]
    reversed_band = per_distance[:, ::-1]
    head_count = per_distance.shape[0]
    tiled = jnp.tile(reversed_band, (1, size_rows + 1))
    start = size_rows - 1
    flat = tiled[:, start : start + size_rows * (span - 1)]
    return flat.reshape(head_count, size_rows, span - 1)[:, :, :size_cols]


def block_scores(query_block, key_block, query_pos, key_pos, bucket_table, bias_heads, score_scale):
    raw_scores = jnp.einsum(
        "qhe,khe->hqk", query_block, key_block, preferred_element_type=jnp.float32
    )
    band = bias_band(
        query_pos[0], key_pos[0], query_block.shape[0], key_block.shape[0], bucket_table, bias_heads
    )
    return raw_scores * score_scale + band


def block_probs(scores, allowed, block_log):
    masked = jnp.where(allowed[None], scores, masked_low)
    return jnp.where(allowed[None], jnp.exp(masked - block_log[:, :, None]), 0.0)


def diagonal_sums(d_scores):
    head_count, size_rows, size_cols = d_scores.shape
    flipped = d_scores[:, :, ::-1]
    padded = jnp.pad(flipped, ((0, 0), (0, 0), (0, size_rows)))
    skewed = padded.reshape(head_count, 2 * size_rows * size_rows)[
        :, : size_rows * (2 * size_rows - 1)
    ]
    skewed = skewed.reshape(head_count, size_rows, 2 * size_rows - 1)
    return jnp.sum(skewed.astype(jnp.float32), axis=1)


def table_terms(d_scores, query_first, key_first, bucket_table, bucket_ids):
    size_rows = d_scores.shape[1]
    per_distance = diagonal_sums(d_scores)
    offsets = (
        jnp.arange(2 * size_rows - 1, dtype=jnp.int32) - (size_rows - 1) + query_first - key_first
    )
    diag_bucket = bucket_table[jnp.clip(offsets, 0, bucket_table.shape[0] - 1)]
    selector = (diag_bucket[:, None] == bucket_ids[None, :]).astype(jnp.float32)
    return jnp.einsum("hc,cb->bh", per_distance, selector, precision=lax.Precision.HIGHEST)


def key_slices(key_index, block_rows, arrays):
    key_start = key_index * block_rows
    return tuple(
        (lax.dynamic_slice_in_dim(item_rows, key_start, block_rows, 0) for item_rows in arrays)
    )


def attend_forward(
    queries, key_rows, value_rows, query_pos, query_seg, key_pos, key_seg, bucket_table, bias_heads
):
    row_count, head_count, head_size = queries.shape
    block_rows = min(512, row_count)
    key_blocks = key_rows.shape[0] // block_rows
    score_scale = head_size ** (-0.5)

    def one_query_block(query_index):

        def first_pass(carried, key_index):
            key_block, value_block, block_key_pos, block_key_seg = key_slices(
                key_index, block_rows, (key_rows, value_rows, key_pos, key_seg)
            )
            allowed = allowed_block(query_pos, query_seg, block_key_pos, block_key_seg)
            row_top, row_total = carried
            scores = block_scores(
                queries, key_block, query_pos, block_key_pos, bucket_table, bias_heads, score_scale
            )
            masked = jnp.where(allowed[None], scores, masked_low)
            new_top = jnp.maximum(row_top, jnp.max(masked, axis=2))
            grown = jnp.where(allowed[None], jnp.exp(masked - new_top[:, :, None]), 0.0)
            return (
                (new_top, row_total * jnp.exp(row_top - new_top) + jnp.sum(grown, axis=2)),
                None,
            )

        start_state = (
            jnp.full((head_count, block_rows), masked_low, jnp.float32),
            jnp.zeros((head_count, block_rows), jnp.float32),
        )
        (row_top, row_total), unused = lax.scan(first_pass, start_state, jnp.arange(key_blocks))
        block_log = row_top + jnp.log(row_total)

        def second_pass(carried, key_index):
            key_block, value_block, block_key_pos, block_key_seg = key_slices(
                key_index, block_rows, (key_rows, value_rows, key_pos, key_seg)
            )
            allowed = allowed_block(query_pos, query_seg, block_key_pos, block_key_seg)
            scores = block_scores(
                queries, key_block, query_pos, block_key_pos, bucket_table, bias_heads, score_scale
            )
            probabilities = block_probs(scores, allowed, block_log).astype(jnp.bfloat16)
            return (
                carried
                + jnp.einsum(
                    "hqk,khe->qhe", probabilities, value_block, preferred_element_type=jnp.float32
                ),
                None,
            )

        start_values = jnp.zeros((block_rows, head_count, head_size), jnp.float32)
        attended, unused = lax.scan(second_pass, start_values, jnp.arange(key_blocks))
        return (attended, block_log)

    attended, log_total = lax.map(one_query_block, jnp.arange(row_count // block_rows))
    attended = attended.reshape(row_count, head_count, head_size)
    log_total = jnp.transpose(log_total, (1, 0, 2)).reshape(head_count, row_count)
    return (attended, log_total)


def attend_backward(
    queries,
    key_rows,
    value_rows,
    d_attended,
    row_delta,
    log_total,
    query_pos,
    query_seg,
    key_pos,
    key_seg,
    bucket_table,
    bias_heads,
    bucket_count,
):
    row_count, head_count, head_size = queries.shape
    block_rows = min(512, row_count)
    key_blocks = key_rows.shape[0] // block_rows
    score_scale = head_size ** (-0.5)
    bucket_ids = jnp.arange(bucket_count, dtype=jnp.int32)

    def one_key_block(carried, key_index):
        d_queries, d_table = carried
        key_block, value_block, block_key_pos, block_key_seg = key_slices(
            key_index, block_rows, (key_rows, value_rows, key_pos, key_seg)
        )
        d_keys = jnp.zeros((block_rows, head_count, head_size), jnp.float32)
        d_values = jnp.zeros((block_rows, head_count, head_size), jnp.float32)
        query_block = queries
        d_block = d_attended
        block_pos = query_pos
        block_log = log_total
        block_delta = row_delta
        allowed = allowed_block(block_pos, query_seg, block_key_pos, block_key_seg)

        def accumulate(
            running,
            query_block=query_block,
            d_block=d_block,
            block_pos=block_pos,
            block_log=block_log,
            block_delta=block_delta,
            allowed=allowed,
        ):
            d_query_block, d_key_acc, d_value_acc, d_table_acc = running
            scores = block_scores(
                query_block,
                key_block,
                block_pos,
                block_key_pos,
                bucket_table,
                bias_heads,
                score_scale,
            )
            probabilities = block_probs(scores, allowed, block_log)
            d_probabilities = jnp.einsum(
                "qhe,khe->hqk", d_block, value_block, preferred_element_type=jnp.float32
            )
            d_scores = (probabilities * (d_probabilities - block_delta[:, :, None])).astype(
                jnp.bfloat16
            )
            d_query_block = (
                d_query_block
                + jnp.einsum(
                    "hqk,khe->qhe", d_scores, key_block, preferred_element_type=jnp.float32
                )
                * score_scale
            )
            d_key_acc = (
                jnp.einsum(
                    "hqk,qhe->khe", d_scores, query_block, preferred_element_type=jnp.float32
                )
                * score_scale
            )
            d_value_acc = jnp.einsum(
                "hqk,qhe->khe",
                probabilities.astype(jnp.bfloat16),
                d_block,
                preferred_element_type=jnp.float32,
            )
            d_table_acc = d_table_acc + table_terms(
                d_scores, block_pos[0], block_key_pos[0], bucket_table, bucket_ids
            )
            return (d_query_block, d_key_acc, d_value_acc, d_table_acc)

        running = (d_queries, d_keys, d_values, d_table)
        running = accumulate(running)
        d_queries = d_queries.at[0:block_rows].set(running[0])
        d_keys = running[1]
        d_values = running[2]
        d_table = running[3]
        return ((d_queries, d_table), (d_keys, d_values))

    start_state = (
        jnp.zeros((row_count, head_count, head_size), jnp.float32),
        jnp.zeros((bucket_count, head_count), jnp.float32),
    )
    (d_queries, d_table), (d_key_blocks, d_value_blocks) = lax.scan(
        one_key_block, start_state, jnp.arange(key_blocks)
    )
    return (d_queries, d_key_blocks, d_value_blocks, d_table)


def per_device(
    tokens,
    segment_ids,
    bucket_table,
    w_qkv,
    w_out,
    w_in,
    w_down,
    gain_one,
    shift_one,
    gain_two,
    shift_two,
    bias_in,
    bias_down,
    rel_bias,
    cotangent,
):
    (
        full_qkv,
        full_out,
        full_in,
        full_down,
        full_gain_one,
        full_shift_one,
        full_gain_two,
        full_shift_two,
        full_bias_in,
        full_bias_down,
    ) = (
        lax.all_gather(w_qkv, "fsdp", axis=0, tiled=True),
        lax.all_gather(w_out, "fsdp", axis=0, tiled=True),
        lax.all_gather(w_in, "fsdp", axis=0, tiled=True),
        lax.all_gather(w_down, "fsdp", axis=0, tiled=True),
        lax.all_gather(gain_one, "fsdp", axis=0, tiled=True),
        lax.all_gather(shift_one, "fsdp", axis=0, tiled=True),
        lax.all_gather(gain_two, "fsdp", axis=0, tiled=True),
        lax.all_gather(shift_two, "fsdp", axis=0, tiled=True),
        lax.all_gather(bias_in, "fsdp", axis=0, tiled=True),
        lax.all_gather(bias_down, "fsdp", axis=0, tiled=True),
    )
    row_count = tokens.shape[1]
    model_width = tokens.shape[2]
    bucket_count = rel_bias.shape[0]
    head_count = rel_bias.shape[1]
    head_size = model_width // head_count
    ctx_place = lax.axis_index("ctx")
    group_start = ctx_place * row_count
    query_pos = group_start + jnp.arange(row_count, dtype=jnp.int32)
    group_seg = segment_ids[0]
    query_seg = lax.dynamic_slice_in_dim(group_seg, group_start, row_count, 0)
    bias_heads = jnp.transpose(rel_bias.astype(jnp.float32))
    inputs = tokens[0].astype(jnp.float32)
    first_norm, first_pull = jax.vjp(
        norm_layer, inputs, full_gain_one.astype(jnp.float32), full_shift_one.astype(jnp.float32)
    )
    first_low = first_norm.astype(jnp.bfloat16)
    packed = jnp.dot(first_low, full_qkv, preferred_element_type=jnp.float32).astype(jnp.bfloat16)
    queries = packed[:, :model_width].reshape(row_count, head_count, head_size)
    own_keys = packed[:, model_width : 2 * model_width]
    own_values = packed[:, 2 * model_width :]
    key_rows, value_rows = (
        lax.all_gather(own_keys, "ctx", axis=0, tiled=True),
        lax.all_gather(own_values, "ctx", axis=0, tiled=True),
    )
    key_pos = jnp.arange(key_rows.shape[0], dtype=jnp.int32)
    key_rows = key_rows.reshape(-1, head_count, head_size)
    value_rows = value_rows.reshape(-1, head_count, head_size)
    attended, log_total = attend_forward(
        queries,
        key_rows,
        value_rows,
        query_pos,
        query_seg,
        key_pos,
        group_seg,
        bucket_table,
        bias_heads,
    )
    attended_flat = attended.reshape(row_count, model_width)
    attended_low = attended_flat.astype(jnp.bfloat16)
    mixed_out = jnp.dot(attended_low, full_out, preferred_element_type=jnp.float32)
    middle = inputs + mixed_out
    second_norm, second_pull = jax.vjp(
        norm_layer, middle, full_gain_two.astype(jnp.float32), full_shift_two.astype(jnp.float32)
    )
    second_low = second_norm.astype(jnp.bfloat16)
    inner_pre = jnp.dot(
        second_low, full_in, preferred_element_type=jnp.float32
    ) + full_bias_in.astype(jnp.float32)
    activated, gelu_pull = jax.vjp(exact_gelu, inner_pre)
    activated_low = activated.astype(jnp.bfloat16)
    result = (
        middle
        + jnp.dot(activated_low, full_down, preferred_element_type=jnp.float32)
        + full_bias_down.astype(jnp.float32)
    )
    output = result.astype(jnp.bfloat16)[None]
    d_result = cotangent[0]
    d_result_full = d_result.astype(jnp.float32)
    grad_down = jnp.einsum("td,tf->df", activated_low, d_result, preferred_element_type=jnp.float32)
    grad_bias_down = jnp.sum(d_result_full, axis=0)
    d_activated = jnp.einsum("tf,df->td", d_result, full_down, preferred_element_type=jnp.float32)
    (d_inner,) = gelu_pull(d_activated)
    d_inner_low = d_inner.astype(jnp.bfloat16)
    grad_bias_in = jnp.sum(d_inner_low.astype(jnp.float32), axis=0)
    grad_in = jnp.einsum("td,tf->df", second_low, d_inner_low, preferred_element_type=jnp.float32)
    d_second = jnp.einsum("tf,df->td", d_inner_low, full_in, preferred_element_type=jnp.float32)
    d_middle_norm, grad_gain_two, grad_shift_two = second_pull(d_second)
    d_middle = d_result_full + d_middle_norm
    d_mixed_low = d_middle.astype(jnp.bfloat16)
    grad_out = jnp.einsum(
        "td,tf->df", attended_low, d_mixed_low, preferred_element_type=jnp.float32
    )
    d_attended = jnp.einsum(
        "tf,df->td", d_mixed_low, full_out, preferred_element_type=jnp.float32
    ).astype(jnp.bfloat16)
    row_delta = jnp.transpose(
        jnp.sum(
            (d_attended.astype(jnp.float32) * attended_flat).reshape(
                row_count, head_count, head_size
            ),
            axis=2,
        )
    )
    d_attended_heads = d_attended.reshape(row_count, head_count, head_size)
    d_queries, d_key_blocks, d_value_blocks, d_table = attend_backward(
        queries,
        key_rows,
        value_rows,
        d_attended_heads,
        row_delta,
        log_total,
        query_pos,
        query_seg,
        key_pos,
        group_seg,
        bucket_table,
        bias_heads,
        bucket_count,
    )
    d_key_all = d_key_blocks.reshape(-1, model_width)
    d_value_all = d_value_blocks.reshape(-1, model_width)
    d_keys_own, d_values_own = (
        lax.psum_scatter(
            d_key_all.astype(jnp.bfloat16), "ctx", scatter_dimension=0, tiled=True
        ).astype(jnp.float32),
        lax.psum_scatter(
            d_value_all.astype(jnp.bfloat16), "ctx", scatter_dimension=0, tiled=True
        ).astype(jnp.float32),
    )
    d_packed = jnp.concatenate(
        [d_queries.reshape(row_count, model_width), d_keys_own, d_values_own], axis=1
    ).astype(jnp.bfloat16)
    grad_qkv = jnp.einsum("td,tf->df", first_low, d_packed, preferred_element_type=jnp.float32)
    d_first = jnp.einsum("tf,df->td", d_packed, full_qkv, preferred_element_type=jnp.float32)
    d_inputs_norm, grad_gain_one, grad_shift_one = first_pull(d_first)
    input_grad = (d_middle + d_inputs_norm).astype(jnp.bfloat16)[None]
    summed = (
        lax.psum(grad_qkv.astype(jnp.bfloat16), "ctx").astype(jnp.float32),
        lax.psum(grad_out.astype(jnp.bfloat16), "ctx").astype(jnp.float32),
        lax.psum(grad_in.astype(jnp.bfloat16), "ctx").astype(jnp.float32),
        lax.psum(grad_down.astype(jnp.bfloat16), "ctx").astype(jnp.float32),
        lax.psum(grad_gain_one.astype(jnp.bfloat16), "ctx").astype(jnp.float32),
        lax.psum(grad_shift_one.astype(jnp.bfloat16), "ctx").astype(jnp.float32),
        lax.psum(grad_gain_two.astype(jnp.bfloat16), "ctx").astype(jnp.float32),
        lax.psum(grad_shift_two.astype(jnp.bfloat16), "ctx").astype(jnp.float32),
        lax.psum(grad_bias_in.astype(jnp.bfloat16), "ctx").astype(jnp.float32),
        lax.psum(grad_bias_down.astype(jnp.bfloat16), "ctx").astype(jnp.float32),
    )
    shards = (
        lax.psum_scatter(summed[0], "fsdp", scatter_dimension=0, tiled=True),
        lax.psum_scatter(summed[1], "fsdp", scatter_dimension=0, tiled=True),
        lax.psum_scatter(summed[2], "fsdp", scatter_dimension=0, tiled=True),
        lax.psum_scatter(summed[3], "fsdp", scatter_dimension=0, tiled=True),
        lax.psum_scatter(summed[4], "fsdp", scatter_dimension=0, tiled=True),
        lax.psum_scatter(summed[5], "fsdp", scatter_dimension=0, tiled=True),
        lax.psum_scatter(summed[6], "fsdp", scatter_dimension=0, tiled=True),
        lax.psum_scatter(summed[7], "fsdp", scatter_dimension=0, tiled=True),
        lax.psum_scatter(summed[8], "fsdp", scatter_dimension=0, tiled=True),
        lax.psum_scatter(summed[9], "fsdp", scatter_dimension=0, tiled=True),
    )
    grad_table = lax.psum(d_table, ("ctx", "fsdp"))
    return (
        output,
        input_grad,
        shards[0],
        shards[1],
        shards[2],
        shards[3],
        shards[4],
        shards[5],
        shards[6],
        shards[7],
        shards[8],
        shards[9],
        grad_table,
    )


def solution(mesh):
    in_specs = (
        P("fsdp", "ctx", None),
        P("fsdp", None),
        P(),
        P("fsdp", None),
        P("fsdp", None),
        P("fsdp", None),
        P("fsdp", None),
        P("fsdp"),
        P("fsdp"),
        P("fsdp"),
        P("fsdp"),
        P("fsdp"),
        P("fsdp"),
        P(),
        P("fsdp", "ctx", None),
    )
    out_specs = (
        P("fsdp", "ctx", None),
        P("fsdp", "ctx", None),
        P("fsdp", None),
        P("fsdp", None),
        P("fsdp", None),
        P("fsdp", None),
        P("fsdp"),
        P("fsdp"),
        P("fsdp"),
        P("fsdp"),
        P("fsdp"),
        P("fsdp"),
        P(),
    )
    return jax.shard_map(
        per_device, mesh=mesh, in_specs=in_specs, out_specs=out_specs, check_vma=False
    )
```

profile of v0, /device:TPU:0, one launch (start us, length us, event | category | flops | bytes accessed | tf_op | source)
XLA Modules:
  0.0 1177.6 jit_solution(7676362515616377456)
XLA Ops:
  14.2 24.2 %all-reduce.13 = (bf16[512]{0:T(512)(128)(2,1)S(1)}, bf16[512]{0:T(512)(128)(2,1)S(1)}, bf16[512]{0:T(512)(128)(2,1)S(1)}, bf16[512]{0:T(512)(128)(2,1)S(1)}, bf16[512]{0:T(512)(128)(2,1)}) all-reduce(bf16[512]{0:T(512)(128)(2,1)S(1)} %dynamic-update-slice.3, ...), channel_id=1, replica_groups=mesh['ctx'=4,'fsdp'=8] {'fsdp'}, use_global_device_ids=true, to_apply=%add.2 | all-reduce | flops 2560 | bytes 10240
  41.3 15.8 %all-gather.7.cloned.1.call-done = bf16[512,1536]{1,0:T(8,128)(2,1)} async-done(((bf16[64,1536]{1,0:T(8,128)(2,1)}), bf16[512,1536]{1,0:T(8,128)(2,1)}) %all-gather.7.cloned.1.call-update) | async-done | bytes 1572880 | tf_op jit(solution)/shard_map/all_gather | solution.py:276
  62.3 18.4 %all-gather = bf16[8,1,256]{2,1,0:T(2,128)(2,1)S(1)} all-gather(bf16[1,1,256]{2,1,0:T(2,128)(2,1)S(1)} %reshape.621), channel_id=1, replica_groups=mesh['ctx'=4,'fsdp'=8] {'fsdp'}, dimensions={0}, use_global_device_ids=true | all-gather | bytes 4608 | tf_op jit(solution)/shard_map/all_gather | solution.py:284
  80.7 34.2 %all_gather.41 = bf16[512,512]{1,0:T(8,128)(2,1)} all-gather(bf16[64,512]{1,0:T(8,128)(2,1)S(1)} %copy-done.24), channel_id=1, replica_groups=mesh['ctx'=4,'fsdp'=8] {'fsdp'}, dimensions={0}, use_global_device_ids=true | all-gather | bytes 589824 | tf_op jit(solution)/shard_map/all_gather | solution.py:277
  117.3 145.4 %while.62 = (s32[]{:T(128)}, f32[8,256]{1,0:T(8,128)S(1)}, f32[8,256]{1,0:T(8,128)S(1)}, s32[4]{0:T(128)S(1)}, s32[1024]{0:T(1024)S(1)}, /*index=5*/s32[256]{0:T...) while((s32[]{:T(128)}, f32[8,256]{1,0:T(8,128)S(1)}, ...), condition=%wide.region_5.6_spmd.clone, body=%wide.region_2.5_spmd.clone.sunk | while | flops 71058680 | bytes 47073720 | solution.py:114
  139.5 8.1 reshape.683
  175.8 8.1 reshape.683
  212.2 8.1 reshape.683
  248.5 8.1 reshape.683
  265.1 149.1 %while.63 = (s32[]{:T(128)}, f32[256,8,64]{0,2,1:T(8,128)}, s32[4]{0:T(128)S(1)}, bf16[1024,8,64]{0,2,1:T(8,128)(2,1)}, s32[1024]{0:T(1024)S(1)}, /*index=5*/s32...) while((s32[]{:T(128)}, f32[256,8,64]{0,2,1:T(8,128)}, ...), condition=%wide.region_7.8_spmd.clone, body=%wide.region_6.7_spmd.clone.sunk | while | flops 137895168 | bytes 48222196 | solution.py:135
  287.6 8.1 reshape.688
  324.8 8.1 reshape.688
  362.0 8.1 reshape.688
  399.2 8.1 reshape.688
  417.4 8.4 multiply_convert_fusion
  433.5 231.7 %while.64 = (s32[]{:T(128)}, f32[256,8,64]{0,2,1:T(8,128)}, f32[32,8]{0,1:T(8,128)S(1)}, bf16[4,256,8,64]{1,3,2,0:T(8,128)(2,1)}, bf16[4,256,8,64]{1,3,2,0:T(8,1...) while((s32[]{:T(128)}, f32[256,8,64]{0,2,1:T(8,128)}, ...), condition=%wide.region_15.16_spmd.clone, body=%wide.region_13.15_spmd.clone.sunk | while | flops 344732384 | bytes 99609160 | solution.py:241
  455.8 8.2 reshape.693
  480.7 8.0 reshape.694
  513.6 8.2 reshape.693
  538.5 8.0 reshape.694
  571.5 8.2 reshape.693
  596.3 8.0 reshape.694
  629.3 8.2 reshape.693
  654.1 8.0 reshape.694
  677.7 12.7 %reduce-scatter.9.cloned.1.call-done = bf16[256,512]{0,1:T(8,128)(2,1)} async-done(((bf16[1024,512]{0,1:T(8,128)(2,1)}), bf16[256,512]{0,1:T(8,128)(2,1)}) %reduce-scatter.9.cloned.1.call-update) | async-done | bytes 262160 | tf_op jit(solution)/shard_map/reduce_scatter | solution.py:393
  690.4 27.6 %reduce-scatter.7.cloned.1.call-done = bf16[256,512]{0,1:T(8,128)(2,1)} async-done(((bf16[1024,512]{0,1:T(8,128)(2,1)}), bf16[256,512]{0,1:T(8,128)(2,1)}) %reduce-scatter.7.cloned.1.call-update) | async-done | bytes 262160 | tf_op jit(solution)/shard_map/reduce_scatter | solution.py:390
  721.0 120.3 %all-reduce.18.cloned.1.call-done = (bf16[512,1536]{1,0:T(8,128)(2,1)}, bf16[512,512]{1,0:T(8,128)(2,1)}, bf16[512,2048]{1,0:T(8,128)(2,1)}, bf16[2048,512]{1,0:T(8,128)(2,1)}) async-done(((bf16[512,1536]{1,0:T(8,128)(2,1)}, bf16[512,512]{1,0:T(8,128)(2,1)}, bf16[512,2048]{1,0:T(8,128)(2,1)}, bf16[2048,512]{1,0:T(8,128)(2,1)}), (bf16[512,1536]{1,0:T(8,128)(2,1)}, bf16[512,512]{1,0:T(8,128)(2,1)}, ...) | async-done | bytes 6291472 | tf_op jit(solution)/shard_map/psum | solution.py:405
  857.0 39.6 %psum.87 = f32[32,8]{0,1:T(8,128)} all-reduce(f32[32,8]{0,1:T(8,128)S(1)} %get-tuple-element.677), channel_id=1, replica_groups=mesh['ctx'=4,'fsdp'=8] {'ctx','fsdp'}, use_global_device_ids=true, to_apply=%region_46.47 | all-reduce | flops 256 | bytes 2048 | tf_op jit(solution)/shard_map/psum | solution.py:428
  907.7 36.4 %all-reduce.12 = (f32[512]{0:T(512)S(1)}, f32[512]{0:T(512)S(1)}, f32[512]{0:T(512)S(1)}, f32[512]{0:T(512)S(1)}, f32[2048]{0:T(1024)S(1)}, /*index=5*/f32[512]{0:T(512)S(1)}) all-reduce(bf16[512]{0:T(512)(128)(2,1)S(1)} %get-tuple-element.1021, ...), channel_id=8, replica_groups=mesh['ctx'=4,'fsdp'=8] {'fsdp'}, use_global_device_ids=true, to_apply=%region_30.31.clone | all-reduce | flops 4608 | bytes 27648
  948.7 38.5 %reduce-scatter.11.cloned.1.call-done = f32[64,1536]{1,0:T(8,128)} async-done(((f32[512,1536]{1,0:T(8,128)}), f32[64,1536]{1,0:T(8,128)}) %reduce-scatter.11.cloned.1.call-update) | async-done | bytes 393232 | tf_op jit(solution)/shard_map/reduce_scatter | solution.py:417
  987.2 91.7 %reduce-scatter.15.cloned.1.call-done = f32[64,2048]{1,0:T(8,128)} async-done(((f32[512,2048]{1,0:T(8,128)}), f32[64,2048]{1,0:T(8,128)}) %reduce-scatter.15.cloned.1.call-update) | async-done | bytes 524304 | tf_op jit(solution)/shard_map/reduce_scatter | solution.py:419
  1078.9 91.7 %reduce-scatter.17.cloned.1.call-done = f32[256,512]{1,0:T(8,128)} async-done(((f32[2048,512]{1,0:T(8,128)}), f32[256,512]{1,0:T(8,128)}) %reduce-scatter.17.cloned.1.call-update) | async-done | bytes 524304 | tf_op jit(solution)/shard_map/reduce_scatter | solution.py:420
  (558 shorter events, 461.5 us)
Async XLA Ops:
  7.2 49.9 %all-gather.7.cloned.1.call-start = ((), (), s32[]{:S(2)}) async-start(), calls=%async_computation.6 | async-start | bytes 1769472 | tf_op jit(solution)/shard_map/all_gather | solution.py:276
  7.9 107.1 %all-gather.11.cloned.1.call-start = ((), (), s32[]{:S(2)}) async-start(), calls=%async_computation.8 | async-start | bytes 1310720 | tf_op jit(solution)/shard_map/all_gather | solution.py:308
  38.4 18.7 %copy-start.36 = (f32[512]{0:T(512)}, f32[512]{0:T(512)S(1)}, u32[]{:S(2)}) copy-start(f32[512]{0:T(512)S(1)} %convert_element_type.171) | copy-start | bytes 6148
  38.4 21.7 %copy-start.26 = (f32[512]{0:T(512)}, f32[512]{0:T(512)S(1)}, u32[]{:S(2)}) copy-start(f32[512]{0:T(512)S(1)} %convert_element_type.170) | copy-start | bytes 6148
  39.5 17.6 %copy-start.28 = (f32[256]{0:T(256)}, f32[256]{0:T(256)S(1)}, u32[]{:S(2)}) copy-start(f32[256]{0:T(256)S(1)} %broadcast_multiply_fusion.1) | copy-start | bytes 3076
  41.3 15.8 %copy-start.30 = (f32[256]{0:T(256)}, f32[256]{0:T(256)S(1)}, u32[]{:S(2)}) copy-start(f32[256]{0:T(256)S(1)} %fusion.76) | copy-start | bytes 3076
  41.3 20.9 %copy-start.43 = (bf16[256]{0:T(256)(128)(2,1)S(1)}, bf16[256]{0:T(256)(128)(2,1)}, u32[]{:S(2)}) copy-start(bf16[256]{0:T(256)(128)(2,1)} %param.36) | copy-start | bytes 1540
  41.3 21.0 %copy-start.35 = (bf16[32,8]{0,1:T(8,128)(2,1)S(1)}, bf16[32,8]{0,1:T(8,128)(2,1)}, u32[]{:S(2)}) copy-start(bf16[32,8]{0,1:T(8,128)(2,1)} %param.38) | copy-start | bytes 1540
  41.3 39.4 %copy-start.24 = (bf16[64,512]{1,0:T(8,128)(2,1)S(1)}, bf16[64,512]{1,0:T(8,128)(2,1)}, u32[]{:S(2)}) copy-start(bf16[64,512]{1,0:T(8,128)(2,1)} %param.29) | copy-start | bytes 196612
  59.2 55.6 %copy-start.25 = (s32[1,1024]{1,0:T(1,128)S(1)}, s32[1,1024]{1,0:T(1,128)}, u32[]{:S(2)}) copy-start(s32[1,1024]{1,0:T(1,128)} %param.26) | copy-start | bytes 12292
  60.1 57.2 %copy-start = (s32[1024]{0:T(1024)S(1)}, s32[1024]{0:T(1024)}, u32[]{:S(2)}) copy-start(s32[1024]{0:T(1024)} %param.27) | copy-start | bytes 12292
  60.2 202.6 %all-gather.9.cloned.1.call-start = ((), (), s32[]{:S(2)}) async-start(), calls=%async_computation.7 | async-start | bytes 1310720 | tf_op jit(solution)/shard_map/all_gather | solution.py:309
  60.9 356.5 %all-gather.13.cloned.1.call-start = ((), (), s32[]{:S(2)}) async-start(), calls=%async_computation.9 | async-start | bytes 2359296 | tf_op jit(solution)/shard_map/all_gather | solution.py:278
  61.5 364.3 %all-gather.15.cloned.1.call-start = ((), (), s32[]{:S(2)}) async-start(), calls=%async_computation.10 | async-start | bytes 2359296 | tf_op jit(solution)/shard_map/all_gather | solution.py:279
  62.1 628.3 %reduce-scatter.9.cloned.1.call-start = ((), (), s32[]{:S(2)}) async-start(), calls=%async_computation.12 | async-start | bytes 1310720 | tf_op jit(solution)/shard_map/reduce_scatter | solution.py:393
  265.1 150.4 %copy-start.7 = (bf16[1,256,512]{2,1,0:T(8,128)(2,1)S(1)}, bf16[1,256,512]{2,1,0:T(8,128)(2,1)}, u32[]{:S(2)}) copy-start(bf16[1,256,512]{2,1,0:T(8,128)(2,1)} %param.25) | copy-start | bytes 786436
  417.1 13.9 %copy-start.5 = (f32[256,512]{1,0:T(8,128)}, f32[256,512]{1,0:T(8,128)S(1)}, u32[]{:S(2)}) copy-start(f32[256,512]{1,0:T(8,128)S(1)} %get-tuple-element.1049) | copy-start | bytes 1572868
  417.4 8.4 copy-start.15
  425.8 4.3 copy-start.39
  668.5 49.5 %reduce-scatter.7.cloned.1.call-start = ((), (), s32[]{:S(2)}) async-start(), calls=%async_computation.11 | async-start | bytes 1310720 | tf_op jit(solution)/shard_map/reduce_scatter | solution.py:390
  671.9 169.4 %all-reduce.18.cloned.1.call-start = ((), (), s32[]{:S(2)}) async-start(), calls=%async_computation.17 | async-start | bytes 12582912 | tf_op jit(solution)/shard_map/psum | solution.py:405
  675.4 42.6 %copy-start.8 = (bf16[1,256,512]{2,1,0:T(8,128)(2,1)S(1)}, bf16[1,256,512]{2,1,0:T(8,128)(2,1)}, u32[]{:S(2)}) copy-start(bf16[1,256,512]{2,1,0:T(8,128)(2,1)} %param.25) | copy-start | bytes 786436
  675.4 42.6 %copy-start.27 = (f32[512]{0:T(512)S(1)}, f32[512]{0:T(512)}, u32[]{:S(2)}) copy-start(f32[512]{0:T(512)} %copy-done.26) | copy-start | bytes 6148
  675.4 42.5 %copy-start.29 = (f32[256]{0:T(256)S(1)}, f32[256]{0:T(256)}, u32[]{:S(2)}) copy-start(f32[256]{0:T(256)} %copy-done.28) | copy-start | bytes 3076
  675.4 42.5 %copy-start.31 = (f32[256]{0:T(256)S(1)}, f32[256]{0:T(256)}, u32[]{:S(2)}) copy-start(f32[256]{0:T(256)} %copy-done.30) | copy-start | bytes 3076
  675.4 42.5 %copy-start.37 = (f32[512]{0:T(512)S(1)}, f32[512]{0:T(512)}, u32[]{:S(2)}) copy-start(f32[512]{0:T(512)} %copy-done.36) | copy-start | bytes 6148
  721.0 227.8 %reduce-scatter.13.cloned.1.call-start = ((), (), s32[]{:S(2)}) async-start(), calls=%async_computation.14 | async-start | bytes 1179648 | tf_op jit(solution)/shard_map/reduce_scatter | solution.py:418
  843.5 143.7 %reduce-scatter.11.cloned.1.call-start = ((), (), s32[]{:S(2)}) async-start(), calls=%async_computation.13 | async-start | bytes 3538944 | tf_op jit(solution)/shard_map/reduce_scatter | solution.py:417
  847.1 231.8 %reduce-scatter.15.cloned.1.call-start = ((), (), s32[]{:S(2)}) async-start(), calls=%async_computation.15 | async-start | bytes 4718592 | tf_op jit(solution)/shard_map/reduce_scatter | solution.py:419
  851.3 319.2 %reduce-scatter.17.cloned.1.call-start = ((), (), s32[]{:S(2)}) async-start(), calls=%async_computation.16 | async-start | bytes 4718592 | tf_op jit(solution)/shard_map/reduce_scatter | solution.py:420
  896.6 3.2 copy-start.42
  899.8 47.9 %copy-start.14 = (f32[256,512]{1,0:T(8,128)S(1)}, f32[256,512]{1,0:T(8,128)}, u32[]{:S(2)}) copy-start(f32[256,512]{1,0:T(8,128)} %copy-done.13) | copy-start | bytes 1572868
  (57 other events, 94.3 us)
Sparse Core Ops, SparseCore 0:
  10.2 46.8 all-gather.6
  60.3 15.5 all-gather.10
  78.0 16.7 all-gather.8
  96.7 50.1 all-gather.12
  148.9 47.7 all-gather.14
  668.6 21.7 reduce-scatter.8
  693.0 24.8 reduce-scatter.6
  721.1 120.1 all-reduce.17
  845.3 63.5 reduce-scatter.12
  913.3 73.8 reduce-scatter.10
  991.8 86.9 reduce-scatter.14
  1082.9 87.6 reduce-scatter.16
where the time goes:
time: 1180 us
  local copies, waits for them, and re-layouts  452 us (38%)
  waiting for transfers between devices  401 us (34%)
  blocking collectives  160 us (14%)
  matrix products  79.6 us (7%)
  other arithmetic  58.3 us (5%)
  between operations  17 us (1%)
    psum x1, waiting for transfers between devices, per_device(): lax.psum(grad_qkv.astype(jnp.bfloat16), 'ctx').astype(jnp.float32)  120 us
    another operation x24, local copies, waits for them, and re-layouts, bias_band(): tiled = jnp.tile(reversed_band, (1, size_rows + 1))  108 us
    reshape x12, local copies, waits for them, and re-layouts, bias_band(): return flat.reshape(head_count, size_rows, span - 1)[:, :, :size_cols]  97.7 us
    reduce_scatter x1, waiting for transfers between devices, per_device(): lax.psum_scatter(summed[3], 'fsdp', scatter_dimension=0, tiled=True)  91.7 us
    reduce_scatter x1, waiting for transfers between devices, per_device(): lax.psum_scatter(summed[2], 'fsdp', scatter_dimension=0, tiled=True)  91.7 us
    slice x12, local copies, waits for them, and re-layouts, bias_band(): flat = tiled[:, start:start + size_rows * (span - 1)]  64.1 us
    unnamed x2, blocking collectives  60.6 us
    psum x1, blocking collectives, per_device(): grad_table = lax.psum(d_table, ('ctx', 'fsdp'))  39.6 us
  transfers between devices with their start and end apart: 12, of which 7 were waited for; matrix products, arithmetic and copies ran while one was open for 28% of the time, Pallas kernels for 0%

commit v1 on v0

v1 whole, which is shorter than its diff:
```python
import functools
import math
from types import SimpleNamespace

import jax
import jax.numpy as jnp
from jax import lax
from jax.experimental import pallas as pl
from jax.experimental.pallas import tpu as pltpu
from jax.sharding import PartitionSpec as P

MESH = pl.DeviceIdType.MESH
F32 = jnp.float32
BF16 = jnp.bfloat16
norm_eps = 1e-05
masked_low = -1e30
CTX = 4
LANES = 128


def mm(left, right, left_dim=1, right_dim=0):
    return lax.dot_general(
        left, right, (((left_dim,), (right_dim,)), ((), ())), preferred_element_type=F32
    )


def norm_stats(rows):
    centre = jnp.mean(rows, axis=-1, keepdims=True)
    centred = rows - centre
    spread = jnp.mean(centred * centred, axis=-1, keepdims=True)
    scale = lax.rsqrt(spread + norm_eps)
    return centred * scale, scale


def norm_back(d_normed, gain_row, hat, scale):
    d_hat = d_normed * gain_row
    mean_d = jnp.mean(d_hat, axis=-1, keepdims=True)
    mean_dh = jnp.mean(d_hat * hat, axis=-1, keepdims=True)
    return scale * (d_hat - mean_d - hat * mean_dh)


class Sizes:
    def __init__(self, n_f, rows, width, ff, group, buckets, heads):
        self.n_f = n_f
        self.half = n_f // 2
        self.rows = rows
        self.width = width
        self.ff = ff
        self.group = group
        self.buckets = buckets
        self.heads = heads
        self.head = width // heads
        self.w_rows = width // n_f
        self.d_rows = ff // n_f
        self.own_ff = ff // CTX
        self.owned = n_f // CTX
        self.blocks = CTX * (CTX + 1) // 2


class Links:
    def __init__(self, send_sems, recv_sems):
        self.send_sems = send_sems
        self.recv_sems = recv_sems
        self.used = 0
        self.pending = []

    def copy(self, src, dst, first, slot, device, index):
        return pltpu.make_async_remote_copy(
            src_ref=src,
            dst_ref=dst,
            send_sem=self.send_sems.at[index],
            recv_sem=self.recv_sems.at[first + slot],
            device_id=device,
            device_id_type=MESH,
        )

    def send(self, src, dst, first, slot, device, guard=None):
        index = self.used
        self.used += 1
        made = self.copy(src, dst, first, slot, device, index)
        if guard is None:
            made.start()
        else:
            pl.when(guard)(made.start)
        self.pending.append((made, guard))

    def wait(self, dst, first, slot, device, guard=None):
        made = self.copy(dst, dst, first, slot, device, 0)
        if guard is None:
            made.wait_recv()
        else:
            pl.when(guard)(made.wait_recv)

    def drain(self):
        for made, guard in self.pending:
            if guard is None:
                made.wait_send()
            else:
                pl.when(guard)(made.wait_send)
        self.pending = []


def count_sends(sizes):
    half, n_f = sizes.half, sizes.n_f
    weights = 3 * ((half - 1) + 1 + (half - 1)) + (half + sizes.owned // 2)
    acts = 3 + 3 + 12 + 9 + 3 + 3
    grads = 2 * (1 + half - 1 + 3) + 2 * (1 + max(1, sizes.owned // 2) + 3)
    return weights + (n_f - 1) + acts + grads + (n_f - 1) + 3 + 16


def layer_kernel(
    sizes,
    tok_in,
    seg_in,
    table_in,
    wqkv_in,
    wout_in,
    win_in,
    wdown_in,
    vec_in0,
    vec_in1,
    vec_in2,
    vec_in3,
    vec_in4,
    bias_in_in,
    rel_in,
    dy_in,
    out_ref,
    dx_ref,
    gqkv_ref,
    gout_ref,
    gin_ref,
    gdown_ref,
    small_ref,
    *scratch_refs,
):
    s, sem = name_scratch(scratch_spec(sizes), scratch_refs[:-3])
    send_sems, recv_sems, own_sems = scratch_refs[-3:]
    n_f, half, rows = sizes.n_f, sizes.half, sizes.rows
    width, w_rows, d_rows, own_ff = sizes.width, sizes.w_rows, sizes.d_rows, sizes.own_ff
    owned = sizes.owned
    head = sizes.head

    c = lax.axis_index("ctx")
    f = lax.axis_index("fsdp")
    side = c // 2
    core = c % 2
    place = f // 2
    par = f % 2
    sib = side * 2 + 1 - core
    opp = (1 - side) * 2 + core
    diag = (1 - side) * 2 + 1 - core
    first_owned = c * owned
    is_owner = (f // owned) == c
    own_slot = f % owned

    def ctx_dev(index):
        return {"ctx": index, "fsdp": f}

    def f_dev(index):
        return {"ctx": c, "fsdp": index}

    partner = 2 * place + 1 - par

    def other_place(step):
        return lax.rem(place + step, half)

    links = Links(send_sems, recv_sems)

    barrier = pltpu.get_barrier_semaphore()
    for step in range(1, CTX):
        pl.semaphore_signal(
            barrier, inc=1, device_id=ctx_dev(lax.rem(c + step, CTX)), device_id_type=MESH
        )
    for step in range(1, n_f):
        pl.semaphore_signal(
            barrier, inc=1, device_id=f_dev(lax.rem(f + step, n_f)), device_id_type=MESH
        )

    own_copies = []

    def fetch(src, dst):
        made = pltpu.make_async_copy(src, dst, own_sems.at[len(own_copies)])
        own_copies.append(made)
        made.start()
        return made

    first_fetches = []
    for part in range(3):
        cols = pl.ds(pl.multiple_of(part * width + c * LANES, LANES), LANES)
        first_fetches.append(
            fetch(wqkv_in.at[:, cols], s.wq.at[f, :, part * LANES : (part + 1) * LANES])
        )
    first_fetches.append(fetch(tok_in, s.tok.at[c]))
    own_cols = pl.ds(pl.multiple_of(c * own_ff, own_ff), own_ff)
    later_fetches = [
        fetch(wout_in, s.wo.at[f]),
        fetch(win_in.at[:, own_cols], s.wi.at[f]),
        fetch(dy_in, s.dy.at[c]),
    ]
    down_fetch = pltpu.make_async_copy(
        wdown_in, s.wd.at[own_slot], own_sems.at[len(own_copies)]
    )
    pl.when(is_owner)(down_fetch.start)
    for at, ref in enumerate((vec_in0, vec_in1, vec_in2, vec_in3, vec_in4)):
        s.vec[f, at : at + 1, 0:w_rows] = ref[...].astype(F32)
    for at in range(bias_in_in.shape[0]):
        size = bias_in_in.shape[1]
        s.vec[f, 5:6, at * size : (at + 1) * size] = bias_in_in[at : at + 1, :].astype(F32)
    for made in first_fetches:
        made.wait()

    pl.semaphore_wait(barrier, CTX - 1 + n_f - 1)

    for step in range(1, n_f):
        to = lax.rem(f + step, n_f)
        links.send(s.vec.at[f], s.vec.at[f], sem.vec, f, f_dev(to))

    def spread(buf, first):
        for step in range(1, half):
            links.send(buf.at[f], buf.at[f], first, f, f_dev(2 * other_place(step) + par))
        links.send(buf.at[f], buf.at[f], first, f, f_dev(partner))

    def pass_on(buf, first):
        for step in range(1, half):
            src = 2 * other_place(step) + par
            links.wait(buf.at[src], first, src, f_dev(src))
            links.send(buf.at[src], buf.at[src], first, src, f_dev(partner))

    def settle(buf, first):
        for step in range(half):
            src = 2 * other_place(step) + 1 - par
            links.wait(buf.at[src], first, src, f_dev(partner))

    spread(s.wq, sem.wq)
    for to in (sib, opp):
        links.send(s.tok.at[c], s.tok.at[c], sem.tok, c, ctx_dev(to))

    ids = lax.broadcasted_iota(jnp.int32, (sizes.buckets, sizes.group), 0)
    onehot = (ids == table_in[...]).astype(BF16)
    s.hot[...] = onehot.astype(F32)
    s.bvec[...] = mm(rel_in[...], onehot)
    for h in range(2):
        row = s.bvec[pl.ds(2 * c + h, 1), :]
        for delta in range(CTX):
            now = row[:, delta * rows : (delta + 1) * rows]
            before = row[:, (delta - 1) * rows : delta * rows] if delta else now
            wide = jnp.broadcast_to(jnp.concatenate([now, before], axis=1), (rows, 2 * rows))
            turned = pltpu.roll(wide, 0, 1, stride=1, stride_axis=0)
            s.tile[h, delta] = turned[:, :rows]
    seg_f = seg_in[...].astype(F32)
    for at in range(CTX):
        piece = jnp.broadcast_to(seg_f[:, at * rows : (at + 1) * rows], (rows, rows))
        s.segk[at] = jnp.transpose(piece)
    key_pos = lax.broadcasted_iota(jnp.int32, (rows, rows), 0)
    query_pos = lax.broadcasted_iota(jnp.int32, (rows, rows), 1)
    for q_at in range(CTX):
        seg_q = jnp.broadcast_to(seg_f[:, q_at * rows : (q_at + 1) * rows], (rows, rows))
        for k_at in range(q_at + 1):
            seg_k = s.segk[k_at]
            allowed = (seg_k == 0.0) | (seg_k == seg_q)
            if q_at == k_at:
                allowed = allowed & (key_pos <= query_pos)
            for h in range(2):
                block = q_at * (q_at + 1) // 2 + k_at
                s.bm[h, block] = jnp.where(allowed, s.tile[h, q_at - k_at], masked_low)

    for step in range(1, n_f):
        src = lax.rem(f + step, n_f)
        links.wait(s.vec.at[src], sem.vec, src, f_dev(src))

    def joined(pieces, count, size):
        total = count * size
        spot = lax.broadcasted_iota(jnp.int32, (size, total), 1) % size
        which = lax.broadcasted_iota(jnp.int32, (size, total), 0)
        spreader = (spot == which).astype(BF16)
        flat = mm(pieces.astype(BF16), spreader)
        owner = lax.broadcasted_iota(jnp.int32, (count, total), 1) // size
        mine = owner == lax.broadcasted_iota(jnp.int32, (count, total), 0)
        return jnp.sum(jnp.where(mine, flat, 0.0), axis=0, keepdims=True)

    for at in range(5):
        s.vrow[at : at + 1, :] = joined(s.vec[:, at, 0:w_rows], n_f, w_rows)
    s.vrow[5:6, :] = joined(s.vec[pl.ds(first_owned, owned), 5, 0:d_rows], owned, d_rows)
    gain_one, shift_one = s.vrow[0:1, :], s.vrow[1:2, :]
    gain_two, shift_two = s.vrow[2:3, :], s.vrow[3:4, :]
    bias_down_row, bias_in_row = s.vrow[4:5, :], s.vrow[5:6, :]

    step_rows = 64

    def row_loop(body, count=rows):
        def run(at, carried):
            body(pl.ds(pl.multiple_of(at * step_rows, step_rows), step_rows))
            return carried

        lax.fori_loop(0, count // step_rows, run, 0)

    def first_norm(chunk):
        def body(part):
            hat, scale = norm_stats(s.tok[chunk, part, :].astype(F32))
            s.fn[chunk, part, :] = (hat * gain_one + shift_one).astype(BF16)

        row_loop(body)

    def whole(buf, count, size, kept):
        if size % 16 == 0:
            return buf[...].reshape(count * size, buf.shape[2])
        for at in range(count):
            kept[at * size : (at + 1) * size, :] = buf[at]
        return kept[...]

    head_rows = lax.broadcasted_iota(jnp.int32, (LANES, rows), 0) // head

    def project(chunk):
        weights = whole(s.wq, n_f, w_rows, s.flat_wq)
        made = mm(s.fn[chunk], weights)
        queries = made[:, 0:LANES].astype(BF16).astype(F32) * (head ** -0.5)
        keys = made[:, LANES : 2 * LANES]
        values = made[:, 2 * LANES : 3 * LANES]
        s.k[chunk] = keys.astype(BF16)
        s.v[chunk] = values.astype(BF16)
        s.kt[chunk] = jnp.transpose(keys).astype(BF16)
        s.vt[chunk] = jnp.transpose(values).astype(BF16)
        turned = jnp.transpose(queries)
        for h in range(2):
            kept = jnp.where(head_rows == h, turned, 0.0)
            s.qt[h, chunk] = kept.astype(BF16)
            s.q[h, chunk] = jnp.transpose(kept).astype(BF16)

    first_norm(c)
    pass_on(s.wq, sem.wq)
    links.wait(s.tok.at[sib], sem.tok, sib, ctx_dev(sib))
    first_norm(sib)
    links.wait(s.tok.at[opp], sem.tok, opp, ctx_dev(opp))
    links.send(s.tok.at[opp], s.tok.at[opp], sem.tok, opp, ctx_dev(sib))
    first_norm(opp)

    for made in later_fetches:
        made.wait()
    pl.when(is_owner)(down_fetch.wait)
    spread(s.wo, sem.wo)
    spread(s.wi, sem.wi)
    down_src = s.wd.at[own_slot]
    for step in range(1, half):
        to = 2 * other_place(step) + par
        links.send(down_src, down_src, sem.wd, own_slot, f_dev(to), is_owner)
    links.send(down_src, down_src, sem.wd, own_slot, f_dev(partner), is_owner)
    for to in (sib, opp):
        links.send(s.dy.at[c], s.dy.at[c], sem.dy, c, ctx_dev(to))

    settle(s.wq, sem.wq)
    project(c)
    project(sib)
    project(opp)
    links.wait(s.tok.at[diag], sem.tok, diag, ctx_dev(sib))
    first_norm(diag)
    project(diag)

    def attend(chunk):
        first_block = chunk * (chunk + 1) // 2

        def score_pass(k_at, tops):
            keys = s.k[k_at]
            grown = []
            for h in range(2):
                scores = mm(keys, s.qt[h, chunk]) + s.bm[h, first_block + k_at]
                s.sc[h, k_at] = scores
                grown.append(jnp.maximum(tops[h], jnp.max(scores, axis=0, keepdims=True)))
            return tuple(grown)

        low = jnp.full((1, rows), masked_low, F32)
        tops = lax.fori_loop(0, chunk + 1, score_pass, (low, low))
        s.acc[...] = jnp.zeros((LANES, rows), F32)

        def value_pass(k_at, sums):
            grown = []
            for h in range(2):
                weights = jnp.exp(s.sc[h, k_at] - tops[h])
                grown.append(sums[h] + jnp.sum(weights, axis=0, keepdims=True))
                rounded = weights.astype(BF16)
                s.e[h, first_block + k_at] = rounded
                part = slice(h * head, (h + 1) * head)
                s.acc[part, :] += mm(s.vt[k_at, part, :], rounded)
            return tuple(grown)

        none = jnp.zeros((1, rows), F32)
        sums = lax.fori_loop(0, chunk + 1, value_pass, (none, none))
        for h in range(2):
            part = slice(h * head, (h + 1) * head)
            inverse = 1.0 / sums[h]
            s.linv[chunk, h : h + 1, :] = inverse
            s.att_t[chunk, part, :] = s.acc[part, :] * inverse
        s.att[c, chunk] = jnp.transpose(s.att_t[chunk]).astype(BF16)

    def att_slot(owner, chunk):
        return owner * CTX + chunk

    def send_att(chunk):
        piece = s.att.at[c, chunk]
        for to in (sib, opp):
            links.send(piece, piece, sem.att, att_slot(c, chunk), ctx_dev(to))

    def wait_att(owner, chunk, via):
        links.wait(s.att.at[owner, chunk], sem.att, att_slot(owner, chunk), ctx_dev(via))

    def pass_att(chunk):
        wait_att(opp, chunk, opp)
        piece = s.att.at[opp, chunk]
        links.send(piece, piece, sem.att, att_slot(opp, chunk), ctx_dev(sib))

    mine = [lax.rem(2 * side + step, CTX) for step in range(CTX)]
    theirs = [lax.rem(2 * (1 - side) + step, CTX) for step in range(CTX)]
    attend(mine[0])
    send_att(mine[0])
    pass_on(s.wo, sem.wo)
    attend(mine[1])
    send_att(mine[1])
    pass_on(s.wi, sem.wi)
    pass_att(theirs[0])
    links.wait(s.dy.at[opp], sem.dy, opp, ctx_dev(opp))
    links.send(s.dy.at[opp], s.dy.at[opp], sem.dy, opp, ctx_dev(sib))
    attend(mine[2])
    send_att(mine[2])
    pass_att(theirs[1])
    for at in range(owned // 2):
        slot = 2 * at + par
        src = first_owned + slot
        away = src != f
        links.wait(s.wd.at[slot], sem.wd, slot, f_dev(src), away)
        links.send(s.wd.at[slot], s.wd.at[slot], sem.wd, slot, f_dev(partner), away)
    attend(mine[3])
    send_att(mine[3])

    settle(s.wo, sem.wo)
    settle(s.wi, sem.wi)
    for at in range(owned // 2):
        slot = 2 * at + 1 - par
        links.wait(s.wd.at[slot], sem.wd, slot, f_dev(partner))
    links.wait(s.dy.at[sib], sem.dy, sib, ctx_dev(sib))
    links.wait(s.dy.at[diag], sem.dy, diag, ctx_dev(sib))
    pass_att(theirs[2])
    pass_att(theirs[3])
    seen = {}

    def gather_att(chunk):
        wait_att(sib, chunk, sib)
        wait_att(diag, chunk, sib)

    def feed(chunk, own):
        gather_att(chunk)
        w_out = whole(s.wo, n_f, w_rows, s.flat_wo)
        mixed = jnp.zeros((rows, width), F32)
        for owner in range(CTX):
            mixed += mm(s.att[owner, chunk], w_out[owner * LANES : (owner + 1) * LANES, :])
        s.mid[...] = mixed + s.tok[chunk].astype(F32)

        def normed(part):
            hat, scale = norm_stats(s.mid[part, :])
            s.sn[chunk, part, :] = (hat * gain_two + shift_two).astype(BF16)

        row_loop(normed)
        w_in = whole(s.wi, n_f, w_rows, s.flat_wi)
        w_down = whole(s.wd, owned, d_rows, None)
        s.inner[...] = mm(s.sn[chunk], w_in)
        s.dact[...] = mm(s.dy[chunk], w_down, 1, 1)

        def gelu(part):
            inner = s.inner[part, :] + bias_in_row
            phi = 0.5 + 0.5 * lax.erf(inner * (2.0 ** -0.5))
            slope = phi + inner * (jnp.exp(-0.5 * inner * inner) * (1.0 / math.sqrt(2.0 * math.pi)))
            s.actv[chunk, part, :] = (inner * phi).astype(BF16)
            s.din[chunk, part, :] = (s.dact[part, :] * slope).astype(BF16)

        row_loop(gelu)
        return mm(s.din[chunk], w_in, 1, 1)

    def scatter_first(group, first, part):
        group[0][...] = part.astype(BF16)
        links.send(group[0], group[1], first[0], 0, ctx_dev(sib))

    def scatter_second(group, first, part):
        links.wait(group[1], first[0], 0, ctx_dev(sib))
        group[2][...] = (part + group[1][...].astype(F32)).astype(BF16)
        links.send(group[2], group[3], first[1], 0, ctx_dev(opp))

    def scatter_third(group, first, part):
        group[4][...] = part.astype(BF16)
        links.send(group[4], group[5], first[2], 0, ctx_dev(sib))

    def scatter_wait(group, first):
        links.wait(group[5], first[2], 0, ctx_dev(sib))
        links.wait(group[3], first[1], 0, ctx_dev(opp))

    def scatter_sum(group, part):
        return group[3][part, :].astype(F32) + group[5][part, :].astype(F32)

    scatter_first(s.rs_s, sem.rs_s, feed(diag, False))
    scatter_second(s.rs_s, sem.rs_s, feed(opp, False))
    scatter_third(s.rs_s, sem.rs_s, feed(sib, False))
    s.dsec[...] = feed(c, True)

    w_down = whole(s.wd, owned, d_rows, None)
    scatter_first(s.rs_o, sem.rs_o, mm(s.actv[diag], w_down))
    scatter_second(s.rs_o, sem.rs_o, mm(s.actv[opp], w_down))
    scatter_third(s.rs_o, sem.rs_o, mm(s.actv[sib], w_down))
    s.outp[...] = s.mid[...] + mm(s.actv[c], w_down) + bias_down_row

    def even_pieces(group, left, right, cols):
        for at in range(width // LANES):
            lhs = left[:, :, at * LANES : (at + 1) * LANES].reshape(CTX * rows, LANES)
            made = mm(lhs, right[...].reshape(CTX * rows, cols), 0, 0).astype(BF16)
            for piece in range(LANES // w_rows):
                to = at * (LANES // w_rows) + piece
                group[0][to % 2, to // 2] = made[piece * w_rows : (piece + 1) * w_rows, :]

    def grad_pair(group, first):
        links.send(
            group[0].at[1 - par], group[1], first[0], 0, f_dev(partner)
        )

    def grad_even_second(group, first):
        links.wait(group[1], first[0], 0, f_dev(partner))
        group[2][...] = (
            group[0][par].astype(F32) + group[1][...].astype(F32)
        ).astype(BF16)
        for step in range(1, half):
            to = other_place(step)
            links.send(
                group[2].at[to], group[3].at[place], first[1], place, f_dev(2 * to + par)
            )

    def grad_even_third(group, first):
        total = group[2][place].astype(F32)
        for step in range(1, half):
            src = other_place(step)
            links.wait(group[3].at[src], first[1], src, f_dev(2 * src + par))
            total += group[3][src].astype(F32)
        group[4][c] = total.astype(BF16)
        for step in range(1, CTX):
            to = lax.rem(c + step, CTX)
            links.send(group[4].at[c], group[4].at[c], first[2], c, ctx_dev(to))

    def grad_even_wait(group, first):
        for step in range(1, CTX):
            src = lax.rem(c + step, CTX)
            links.wait(group[4].at[src], first[2], src, ctx_dev(src))

    own_half = owned // 2

    def grad_odd_second(group, first):
        links.wait(group[1], first[0], 0, f_dev(partner))
        group[2][...] = (
            group[0][par].astype(F32) + group[1][...].astype(F32)
        ).astype(BF16)
        for at in range(own_half):
            to = c * own_half + at
            links.send(
                group[2].at[at],
                group[3].at[place],
                first[1],
                place,
                f_dev(2 * to + par),
                to != place,
            )

    owner_ctx = f // owned

    def grad_odd_third(group, first):
        for step in range(1, half):
            src = other_place(step)
            links.wait(group[3].at[src], first[1], src, f_dev(2 * src + par), is_owner)

        @pl.when(is_owner)
        def add_up():
            total = group[2][lax.rem(place, own_half)].astype(F32)
            for step in range(1, half):
                total += group[3][other_place(step)].astype(F32)
            group[4][...] = total.astype(BF16)

        for step in range(1, CTX):
            to = lax.rem(c + step, CTX)
            links.send(group[4], group[4], first[2], 0, ctx_dev(to), is_owner)

    def grad_odd_wait(group, first):
        links.wait(group[4], first[2], 0, ctx_dev(owner_ctx), jnp.logical_not(is_owner))

    def down_pieces():
        for at in range(own_ff // LANES):
            lhs = s.actv[:, :, at * LANES : (at + 1) * LANES].reshape(CTX * rows, LANES)
            made = mm(lhs, s.dy[...].reshape(CTX * rows, width), 0, 0).astype(BF16)
            low, high = at * LANES, (at + 1) * LANES
            for slot in range(owned):
                left, right = max(low, slot * d_rows), min(high, (slot + 1) * d_rows)
                if left < right:
                    inside = slice(left - slot * d_rows, right - slot * d_rows)
                    s.gd[0][slot % 2, slot // 2, inside, :] = made[left - low : right - low, :]

    down_pieces()
    grad_pair(s.gd, sem.gd)
    even_pieces(s.gi, s.sn, s.din, own_ff)
    grad_pair(s.gi, sem.gi)

    scatter_wait(s.rs_s, sem.rs_s)

    def zero_sums():
        s.vg[...] = jnp.zeros_like(s.vg)

    zero_sums()

    def second_back(part):
        hat, scale = norm_stats(s.mid[part, :])
        d_second = s.dsec[part, :] + scatter_sum(s.rs_s, part)
        d_result = s.dy[c, part, :].astype(F32)
        d_middle = d_result + norm_back(d_second, gain_two, hat, scale)
        s.dmid[part, :] = d_middle
        s.dmx[c, part, :] = d_middle.astype(BF16)
        s.vg[2:3, :] += jnp.sum(d_second * hat, axis=0, keepdims=True)
        s.vg[3:4, :] += jnp.sum(d_second, axis=0, keepdims=True)
        s.vg[4:5, :] += jnp.sum(d_result, axis=0, keepdims=True)

    row_loop(second_back)
    d_att = mm(whole(s.wo, n_f, w_rows, s.flat_wo), s.dmx[c], 1, 1)
    s.dat_out[...] = d_att.astype(BF16).reshape(CTX, LANES, rows)
    for to in (opp, diag, sib):
        links.send(s.dat_out.at[to], s.dat.at[c], sem.dat, c, ctx_dev(to))
    s.dat[c] = s.dat_out[c]
    for to in (sib, opp):
        links.send(s.dmx.at[c], s.dmx.at[c], sem.dmx, c, ctx_dev(to))
    grad_even_second(s.gi, sem.gi)
    grad_odd_second(s.gd, sem.gd)
    for at in range(CTX):
        def bias_rows(part, at=at):
            s.vg[5:6, :] += jnp.sum(s.din[at, part, :].astype(F32), axis=0, keepdims=True)

        row_loop(bias_rows)
    scatter_wait(s.rs_o, sem.rs_o)
    out_ref[...] = (
        s.outp[...] + s.rs_o[3][...].astype(F32) + s.rs_o[5][...].astype(F32)
    ).astype(BF16)

    for src in (sib, opp, diag):
        links.wait(s.dat.at[src], sem.dat, src, ctx_dev(src))
    for at in range(CTX):
        got = s.dat[at].astype(F32)
        for h in range(2):
            part = slice(h * head, (h + 1) * head)
            scaled = (got * s.linv[at, h : h + 1, :]).astype(BF16)
            kept = jnp.where(head_rows == h, scaled.astype(F32), 0.0)
            s.dat_t[h, at] = kept.astype(BF16)
            s.dat_n[h, at] = jnp.transpose(kept).astype(BF16)
            s.delta[at, h : h + 1, :] = jnp.sum(
                kept[part, :] * s.att_t[at, part, :], axis=0, keepdims=True
            )
        s.dqt[at] = jnp.zeros((LANES, rows), F32)
    s.dbm[...] = jnp.zeros_like(s.dbm)

    def key_block(k_at, carried):
        s.dk[...] = jnp.zeros((rows, LANES), F32)
        s.dv[...] = jnp.zeros((rows, LANES), F32)

        def query_block(q_at, inner_carried):
            block = q_at * (q_at + 1) // 2 + k_at
            values = s.v[k_at]
            for h in range(2):
                part = slice(h * head, (h + 1) * head)
                d_probs = mm(values, s.dat_t[h, q_at])
                rounded = s.e[h, block]
                d_scores = rounded.astype(F32) * (d_probs - s.delta[q_at, h : h + 1, :])
                s.dbm[h, q_at - k_at] += d_scores
                low = d_scores.astype(BF16)
                s.dk[...] += mm(low, s.q[h, q_at])
                s.dv[...] += mm(rounded, s.dat_n[h, q_at])
                s.dqt[q_at, part, :] += mm(s.kt[k_at, part, :], low)
            return inner_carried

        lax.fori_loop(k_at, CTX, query_block, 0)
        s.dp[k_at, :, LANES : 2 * LANES] = s.dk[...].astype(BF16)
        s.dp[k_at, :, 2 * LANES : 3 * LANES] = s.dv[...].astype(BF16)
        return carried

    lax.fori_loop(0, CTX, key_block, 0)
    for at in range(CTX):
        s.dp[at, :, 0:LANES] = (jnp.transpose(s.dqt[at]) * (head ** -0.5)).astype(BF16)

    w_qkv = whole(s.wq, n_f, w_rows, s.flat_wq)
    scatter_first(s.rs_f, sem.rs_f, mm(s.dp[diag], w_qkv, 1, 1))
    scatter_second(s.rs_f, sem.rs_f, mm(s.dp[opp], w_qkv, 1, 1))
    even_pieces(s.gq, s.fn, s.dp, 3 * LANES)
    grad_pair(s.gq, sem.gq)
    scatter_third(s.rs_f, sem.rs_f, mm(s.dp[sib], w_qkv, 1, 1))
    s.dsec[...] = mm(s.dp[c], w_qkv, 1, 1)

    links.wait(s.dmx.at[opp], sem.dmx, opp, ctx_dev(opp))
    links.send(s.dmx.at[opp], s.dmx.at[opp], sem.dmx, opp, ctx_dev(sib))
    grad_even_third(s.gi, sem.gi)
    grad_odd_third(s.gd, sem.gd)
    grad_even_second(s.gq, sem.gq)
    links.wait(s.dmx.at[sib], sem.dmx, sib, ctx_dev(sib))
    links.wait(s.dmx.at[diag], sem.dmx, diag, ctx_dev(sib))
    made = jnp.zeros((LANES, width), F32)
    for at in range(CTX):
        made += mm(s.att_t[at].astype(BF16), s.dmx[at])
    for slot in range(owned):
        s.go[0][slot % 2, slot // 2] = made[slot * w_rows : (slot + 1) * w_rows, :].astype(BF16)
    grad_pair(s.go, sem.go)

    for h in range(2):
        pieces = []
        for delta in range(CTX):
            block = s.dbm[h, delta]
            wide = jnp.concatenate([block, jnp.zeros((rows, rows), F32)], axis=1)
            count = rows
            while count > 1:
                count //= 2
                turned = pltpu.roll(wide[count : 2 * count, :], 2 * rows - count, 1)
                wide = wide[0:count, :] + turned
            pieces.append(wide)
        total = []
        for delta in range(CTX):
            here = pieces[delta][:, 0:rows]
            if delta + 1 < CTX:
                here = here + pieces[delta + 1][:, rows : 2 * rows]
            total.append(here)
        dist = jnp.concatenate(total, axis=1)
        sums = lax.dot_general(
            jnp.broadcast_to(dist, (8, sizes.group)),
            s.hot[...],
            (((1,), (1,)), ((), ())),
            preferred_element_type=F32,
            precision=lax.Precision.HIGHEST,
        )
        line = lax.broadcasted_iota(jnp.int32, sums.shape, 0)
        s.vg[8:16, 0 : sizes.buckets] += jnp.where(line == 2 * c + h, sums, 0.0)

    scatter_wait(s.rs_f, sem.rs_f)

    def first_back(part):
        hat, scale = norm_stats(s.tok[c, part, :].astype(F32))
        d_first = s.dsec[part, :] + scatter_sum(s.rs_f, part)
        d_x = s.dmid[part, :] + norm_back(d_first, gain_one, hat, scale)
        dx_ref[part, :] = d_x.astype(BF16)
        s.vg[0:1, :] += jnp.sum(d_first * hat, axis=0, keepdims=True)
        s.vg[1:2, :] += jnp.sum(d_first, axis=0, keepdims=True)

    row_loop(first_back)
    s.vgf[f] = s.vg[...]
    for step in range(1, n_f):
        to = lax.rem(f + step, n_f)
        links.send(s.vg, s.vgf.at[f], sem.vgf, f, f_dev(to))
    grad_odd_second(s.go, sem.go)
    grad_even_third(s.gq, sem.gq)
    for step in range(1, n_f):
        src = lax.rem(f + step, n_f)
        links.wait(s.vgf.at[src], sem.vgf, src, f_dev(src))
    s.vgc[c] = jnp.sum(s.vgf[...], axis=0)
    for step in range(1, CTX):
        to = lax.rem(c + step, CTX)
        links.send(s.vgc.at[c], s.vgc.at[c], sem.vgc, c, ctx_dev(to))
    grad_odd_third(s.go, sem.go)

    grad_even_wait(s.gi, sem.gi)
    gin_ref[...] = s.gi[4][...]
    grad_odd_wait(s.gd, sem.gd)
    gdown_ref[...] = s.gd[4][...]
    grad_even_wait(s.gq, sem.gq)
    gqkv_ref[...] = s.gq[4][...]
    grad_odd_wait(s.go, sem.go)
    gout_ref[...] = s.go[4][...]
    for step in range(1, CTX):
        src = lax.rem(c + step, CTX)
        links.wait(s.vgc.at[src], sem.vgc, src, ctx_dev(src))
    total = jnp.sum(s.vgc[...], axis=0)
    small_ref[0:8, :] = pltpu.roll(total[0:8, :], lax.rem(width - f * w_rows, width), 1)
    hidden = pltpu.roll(s.vgc[owner_ctx, 0:8, :], lax.rem(own_ff - own_slot * d_rows, own_ff), 1)
    small_ref[5:6, :] = hidden[5:6, :]
    small_ref[8:16, :] = total[8:16, :]
    links.drain()


def finish_kernel(
    sizes,
    out_in,
    dx_in,
    gqkv_in,
    gout_in,
    gin_in,
    gdown_in,
    small_in,
    out_ref,
    dx_ref,
    gqkv_ref,
    gout_ref,
    gin_ref,
    gdown_ref,
    gg1_ref,
    gs1_ref,
    gg2_ref,
    gs2_ref,
    gbi_ref,
    gbd_ref,
    grel_ref,
    gqkv,
    gout,
    gin,
    gdown,
    gqkv_low,
    gout_low,
    gin_low,
    gdown_low,
    out_low,
    dx_low,
    sems,
):
    made = []

    def start(src, dst):
        copy = pltpu.make_async_copy(src, dst, sems.at[len(made)])
        copy.start()
        made.append(copy)
        return copy

    loads = [
        start(gdown_in, gdown_low),
        start(gin_in, gin_low),
        start(gqkv_in, gqkv_low),
        start(gout_in, gout_low),
    ]
    loads += [start(out_in, out_low), start(dx_in, dx_low)]
    width, own_ff = sizes.width, sizes.own_ff
    loads[0].wait()
    gdown[...] = gdown_low[...].astype(F32)
    stores = [start(gdown, gdown_ref)]
    loads[1].wait()
    for at in range(CTX):
        gin[:, at * own_ff : (at + 1) * own_ff] = gin_low[at].astype(F32)
    stores.append(start(gin, gin_ref))
    loads[2].wait()
    for at in range(CTX):
        for part in range(3):
            low = part * width + at * LANES
            gqkv[:, low : low + LANES] = gqkv_low[at, :, part * LANES : (part + 1) * LANES].astype(F32)
    stores.append(start(gqkv, gqkv_ref))
    loads[3].wait()
    gout[...] = gout_low[...].astype(F32)
    stores.append(start(gout, gout_ref))
    loads[4].wait()
    stores.append(start(out_low, out_ref))
    loads[5].wait()
    stores.append(start(dx_low, dx_ref))
    for at, ref in enumerate((gg1_ref, gs1_ref, gg2_ref, gs2_ref, gbd_ref)):
        ref[...] = small_in[at : at + 1, 0 : sizes.w_rows]
    size = gbi_ref.shape[1]
    for at in range(gbi_ref.shape[0]):
        gbi_ref[at : at + 1, :] = small_in[5:6, at * size : (at + 1) * size]
    grel_ref[...] = small_in[8:16, 0 : sizes.buckets]
    for copy in stores:
        copy.wait()


def scratch_spec(z):
    rows, width, group = z.rows, z.width, z.group
    own_half = z.owned // 2
    blocks = CTX * (CTX + 1) // 2
    act = (CTX, rows, width)
    hidden = (CTX, rows, z.own_ff)
    tall = (CTX, rows, LANES)
    wide = (CTX, LANES, rows)
    squares = (2, CTX, rows, rows)

    def scatter():
        flat = ((rows, width), BF16)
        landing = ((rows, width), BF16, 1)
        return [flat, landing, flat, landing, flat, landing]

    def even(cols):
        part = (z.half, z.w_rows, cols)
        return [
            ((2,) + part, BF16),
            (part, BF16, 1),
            (part, BF16),
            (part, BF16, z.half),
            ((CTX, z.w_rows, cols), BF16, CTX),
        ]

    def odd(size):
        part = (own_half, size, width)
        return [
            ((2,) + part, BF16),
            (part, BF16, 1),
            (part, BF16),
            ((z.half, size, width), BF16, z.half),
            ((size, width), BF16, 1),
        ]

    spec = dict(
        tok=(act, BF16, CTX),
        dy=(act, BF16, CTX),
        fn=(act, BF16),
        wq=((z.n_f, z.w_rows, 3 * LANES), BF16, z.n_f),
        wo=((z.n_f, z.w_rows, width), BF16, z.n_f),
        wi=((z.n_f, z.w_rows, z.own_ff), BF16, z.n_f),
        wd=((z.owned, z.d_rows, width), BF16, z.owned),
        vec=((z.n_f, 8, max(z.d_rows, LANES)), F32, z.n_f),
        vrow=((8, width), F32),
        hot=((z.buckets, group), F32),
        bvec=((8, group), F32),
        tile=(squares, F32),
        segk=((CTX, rows, rows), F32),
        bm=((2, blocks, rows, rows), F32),
        k=(tall, BF16),
        v=(tall, BF16),
        kt=(wide, BF16),
        vt=(wide, BF16),
        qt=((2,) + wide, BF16),
        q=((2,) + tall, BF16),
        sc=(squares, F32),
        e=((2, blocks, rows, rows), BF16),
        acc=((LANES, rows), F32),
        linv=((CTX, 8, rows), F32),
        att_t=(wide, F32),
        att=((CTX,) + tall, BF16, CTX * CTX),
        mid=((rows, width), F32),
        sn=(act, BF16),
        inner=((rows, z.own_ff), F32),
        dact=((rows, z.own_ff), F32),
        actv=(hidden, BF16),
        din=(hidden, BF16),
        dsec=((rows, width), F32),
        outp=((rows, width), F32),
        dmid=((rows, width), F32),
        dmx=(act, BF16, CTX),
        dat_out=(wide, BF16),
        dat=(wide, BF16, CTX),
        dat_t=((2,) + wide, BF16),
        dat_n=((2,) + tall, BF16),
        delta=((CTX, 8, rows), F32),
        dqt=(wide, F32),
        dbm=(squares, F32),
        dk=((rows, LANES), F32),
        dv=((rows, LANES), F32),
        dp=((CTX, rows, 3 * LANES), BF16),
        vg=((16, width), F32),
        vgf=((z.n_f, 16, width), F32, z.n_f),
        vgc=((CTX, 16, width), F32, CTX),
        rs_s=scatter(),
        rs_o=scatter(),
        rs_f=scatter(),
        gq=even(3 * LANES),
        gi=even(z.own_ff),
        go=odd(z.w_rows),
        gd=odd(z.d_rows),
    )
    if z.w_rows % 16:
        spec.update(
            flat_wq=((width, 3 * LANES), BF16),
            flat_wo=((width, width), BF16),
            flat_wi=((width, z.own_ff), BF16),
        )
    else:
        spec.update(flat_wq=((8, LANES), BF16), flat_wo=((8, LANES), BF16), flat_wi=((8, LANES), BF16))
    return spec


def scratch_items(spec):
    for item in spec.values():
        if isinstance(item, list):
            yield from item
        else:
            yield item


def name_scratch(spec, refs):
    refs = iter(refs)
    by_name, first, used = {}, {}, 0
    for name, item in spec.items():
        entries = item if isinstance(item, list) else [item]
        held, starts = [], []
        for entry in entries:
            held.append(next(refs))
            if len(entry) > 2:
                starts.append(used)
                used += entry[2]
        by_name[name] = held if isinstance(item, list) else held[0]
        if starts:
            first[name] = starts if isinstance(item, list) else starts[0]
    return SimpleNamespace(**by_name), SimpleNamespace(**first)


def per_device(
    n_f,
    tokens,
    segment_ids,
    bucket_table,
    w_qkv,
    w_out,
    w_in,
    w_down,
    gain_one,
    shift_one,
    gain_two,
    shift_two,
    bias_in,
    bias_down,
    rel_bias,
    cotangent,
):
    sizes = Sizes(
        n_f,
        tokens.shape[1],
        tokens.shape[2],
        w_in.shape[1],
        segment_ids.shape[1],
        rel_bias.shape[0],
        rel_bias.shape[1],
    )
    rows, width, w_rows, d_rows = sizes.rows, sizes.width, sizes.w_rows, sizes.d_rows
    vmem = pl.BlockSpec(memory_space=pltpu.VMEM)
    far = pl.BlockSpec(memory_space=pltpu.HBM)
    spec = scratch_spec(sizes)
    n_recv = sum(item[2] for item in scratch_items(spec) if len(item) > 2)
    bias_shape = (max(1, d_rows // LANES), min(LANES, d_rows))
    shaped = jax.ShapeDtypeStruct
    made = pl.pallas_call(
        functools.partial(layer_kernel, sizes),
        out_shape=[
            shaped((rows, width), BF16),
            shaped((rows, width), BF16),
            shaped((CTX, w_rows, 3 * LANES), BF16),
            shaped((w_rows, width), BF16),
            shaped((CTX, w_rows, sizes.own_ff), BF16),
            shaped((d_rows, width), BF16),
            shaped((16, width), F32),
        ],
        in_specs=[far, vmem, vmem] + [far] * 4 + [vmem] * 7 + [far],
        out_specs=[vmem] * 7,
        scratch_shapes=[pltpu.VMEM(item[0], item[1]) for item in scratch_items(spec)]
        + [
            pltpu.SemaphoreType.DMA((count_sends(sizes),)),
            pltpu.SemaphoreType.DMA((n_recv,)),
            pltpu.SemaphoreType.DMA((8,)),
        ],
        compiler_params=pltpu.CompilerParams(
            collective_id=0, has_side_effects=True, vmem_limit_bytes=60 * 1024 * 1024
        ),
        name="layer",
    )(
        tokens[0],
        segment_ids,
        bucket_table[None],
        w_qkv,
        w_out,
        w_in,
        w_down,
        gain_one[None],
        shift_one[None],
        gain_two[None],
        shift_two[None],
        bias_down[None],
        bias_in.reshape(bias_shape),
        jnp.transpose(rel_bias),
        cotangent[0],
    )
    outs = [
        ((rows, width), BF16),
        ((rows, width), BF16),
        ((w_rows, 3 * width), F32),
        ((w_rows, width), F32),
        ((w_rows, sizes.ff), F32),
        ((d_rows, width), F32),
        ((1, w_rows), F32),
        ((1, w_rows), F32),
        ((1, w_rows), F32),
        ((1, w_rows), F32),
        (bias_shape, F32),
        ((1, w_rows), F32),
        ((sizes.heads, sizes.buckets), F32),
    ]
    done = pl.pallas_call(
        functools.partial(finish_kernel, sizes),
        out_shape=[shaped(shape, kind) for shape, kind in outs],
        in_specs=[far] * 6 + [vmem],
        out_specs=[far] * 6 + [vmem] * 7,
        scratch_shapes=[pltpu.VMEM(shape, kind) for shape, kind in outs[2:6]]
        + [pltpu.VMEM(item.shape, item.dtype) for item in made[2:6] + made[0:2]]
        + [pltpu.SemaphoreType.DMA((12,))],
        compiler_params=pltpu.CompilerParams(vmem_limit_bytes=60 * 1024 * 1024),
        name="finish",
    )(*made)
    return (
        done[0][None],
        done[1][None],
        done[2],
        done[3],
        done[4],
        done[5],
        done[6][0],
        done[7][0],
        done[8][0],
        done[9][0],
        done[10].reshape(-1),
        done[11][0],
        jnp.transpose(done[12]),
    )


def solution(mesh):
    by_f, by_both = P("fsdp"), P("fsdp", "ctx", None)
    in_specs = (by_both, by_f, P()) + (by_f,) * 10 + (P(), by_both)
    out_specs = (by_both, by_both) + (by_f,) * 10 + (P(),)
    return jax.shard_map(
        functools.partial(per_device, mesh.shape["fsdp"]),
        mesh=mesh,
        in_specs=in_specs,
        out_specs=out_specs,
        check_vma=False,
    )
```

time: 1180 us -> 112 us (0.09)
  local copies, waits for them, and re-layouts: 452 us -> 0 us
  waiting for transfers between devices: 401 us -> 0 us
  blocking collectives: 160 us -> 0 us
  Pallas kernels: 0 us -> 111 us
  matrix products: 79.6 us -> 0 us
  other arithmetic: 58.3 us -> 0 us
  between operations: 17 us -> 0.82 us
    reduce_scatter x6 -> x0, waiting for transfers between devices: 262 us -> none  [the longest x1 91.7 us: per_device(): lax.psum_scatter(summed[3], 'fsdp', scatter_dimension=0, tiled=True)]
    psum x1 -> x0, waiting for transfers between devices: 120 us -> none  [per_device(): lax.psum(grad_qkv.astype(jnp.bfloat16), 'ctx').astype(jnp.float32)]
    pallas_call x0 -> x2, Pallas kernels: none -> 111 us  [the longest x1 107 us: per_device(): pl.pallas_call(functools.partial(layer_kernel, sizes), out_shape=[shaped(...]
    another operation x25 -> x0, local copies, waits for them, and re-layouts: 109 us -> none  [the longest x24 108 us: bias_band(): tiled = jnp.tile(reversed_band, (1, size_rows + 1))]
    reshape x12 -> x0, local copies, waits for them, and re-layouts: 97.7 us -> none  [bias_band(): return flat.reshape(head_count, size_rows, span - 1)[:, :, :size_cols]]
    slice x62 -> x0, local copies, waits for them, and re-layouts: 96.5 us -> none  [the longest x12 64.1 us: bias_band(): flat = tiled[:, start:start + size_rows * (span - 1)]]
    dot_general x44 -> x0, matrix products: 79.6 us -> none  [the longest x8 19.2 us: block_scores(): jnp.einsum('qhe,khe->hqk', query_block, key_block, preferred_element_type...]
    unnamed x2 -> x0, blocking collectives: 60.6 us -> none
  transfers between devices with their start and end apart: 12 -> 0, of which waited for: 7 -> 0; matrix products, arithmetic and copies ran while one was open for 28% -> 0% of each run, Pallas kernels for 0% -> 0%
where the time goes in v1:
time: 112 us
  Pallas kernels  111 us (99%)
    pallas_call x1, Pallas kernels, per_device(): pl.pallas_call(functools.partial(layer_kernel, sizes), out_shape=[shaped(...  107 us
    pallas_call x1, Pallas kernels, per_device(): pl.pallas_call(functools.partial(finish_kernel, sizes), out_shape=[shaped...  3.78 us

profile of v1, /device:TPU:0, one launch (start us, length us, event | category | flops | bytes accessed | tf_op | source)
XLA Modules:
  0.0 111.7 jit_solution(4659461421685805807)
XLA Ops:
  0.7 107.1 %layer.1 = (bf16[256,512]{1,0:T(8,128)(2,1)}, bf16[256,512]{1,0:T(8,128)(2,1)}, bf16[4,64,384]{2,1,0:T(8,128)(2,1)}, bf16[64,512]{1,0:T(8,128)(2,1)}, bf16[4,64,...) custom-call(bf16[256,512]{1,0:T(8,128)(2,1)} %bitcast.19, s32[1,1024]{1,0:T(1,128)} %seg_in.1, ...), custom_call_target="tpu_custom_call" | custom-call | tf_op jit(solution)/shard_map/layer/pallas_call | solution.py:1023
  107.8 3.8 %finish.1 = (bf16[256,512]{1,0:T(8,128)(2,1)}, bf16[256,512]{1,0:T(8,128)(2,1)}, f32[64,1536]{1,0:T(8,128)}, f32[64,512]{1,0:T(8,128)}, f32[64,2048]{1,0:T(8,128...) custom-call(bf16[256,512]{1,0:T(8,128)(2,1)} %get-tuple-element.33.o, ...), custom_call_target="tpu_custom_call" | custom-call | tf_op jit(solution)/shard_map/finish/pallas_call | solution.py:1078

commit v2 on v1

v2 whole, which is shorter than its diff:
```python
import functools
import math
from types import SimpleNamespace

import jax
import jax.numpy as jnp
from jax import lax
from jax.experimental import pallas as pl
from jax.experimental.pallas import tpu as pltpu
from jax.sharding import PartitionSpec as P

MESH = pl.DeviceIdType.MESH
F32 = jnp.float32
BF16 = jnp.bfloat16
norm_eps = 1e-05
masked_low = -1e30
CTX = 4
LANES = 128


def mm(left, right, left_dim=1, right_dim=0):
    return lax.dot_general(
        left, right, (((left_dim,), (right_dim,)), ((), ())), preferred_element_type=F32
    )


def norm_stats(rows):
    centre = jnp.mean(rows, axis=-1, keepdims=True)
    centred = rows - centre
    spread = jnp.mean(centred * centred, axis=-1, keepdims=True)
    scale = lax.rsqrt(spread + norm_eps)
    return centred * scale, scale


def norm_back(d_normed, gain_row, hat, scale):
    d_hat = d_normed * gain_row
    mean_d = jnp.mean(d_hat, axis=-1, keepdims=True)
    mean_dh = jnp.mean(d_hat * hat, axis=-1, keepdims=True)
    return scale * (d_hat - mean_d - hat * mean_dh)


class Sizes:
    def __init__(self, n_f, rows, width, ff, group, buckets, heads):
        self.n_f = n_f
        self.half = n_f // 2
        self.rows = rows
        self.width = width
        self.ff = ff
        self.group = group
        self.buckets = buckets
        self.heads = heads
        self.head = width // heads
        self.w_rows = width // n_f
        self.d_rows = ff // n_f
        self.own_ff = ff // CTX
        self.part = self.d_rows // CTX
        self.owned = n_f // CTX
        self.blocks = CTX * (CTX + 1) // 2


class Links:
    def __init__(self, send_sems, recv_sems):
        self.send_sems = send_sems
        self.recv_sems = recv_sems
        self.used = 0
        self.pending = []

    def copy(self, src, dst, index, arrival, device):
        return pltpu.make_async_remote_copy(
            src_ref=src,
            dst_ref=dst,
            send_sem=self.send_sems.at[index],
            recv_sem=self.recv_sems.at[arrival],
            device_id=device,
            device_id_type=MESH,
        )

    def send(self, src, dst, arrival, device):
        self.copy(src, dst, self.used, arrival, device).start()
        self.pending.append((src, self.used, device))
        self.used += 1

    def send_all(self, pairs, arrival, devices, size):
        for (src, dst), device in zip(pairs, devices):
            self.copy(src, dst, self.used, arrival, device).start()
        self.pending.append((size, self.used, devices[0]))
        self.used += 1

    def wait(self, dst, arrival, device):
        self.copy(dst, dst, 0, arrival, device).wait_recv()

    def drain(self):
        for src, index, device in self.pending:
            self.copy(src, src, index, 0, device).wait_send()
        self.pending = []


SENDS = 96


def layer_kernel(
    sizes,
    tok_in,
    seg_in,
    table_in,
    wqkv_in,
    wout_in,
    win_in,
    wdown_in,
    vec_in0,
    vec_in1,
    vec_in2,
    vec_in3,
    vec_in4,
    bias_in_in,
    rel_in,
    dy_in,
    out_ref,
    dx_ref,
    gqk_ref,
    gv_ref,
    gout_ref,
    gin_ref,
    gdown_ref,
    small_ref,
    *scratch_refs,
):
    s, sem = name_scratch(scratch_spec(sizes), scratch_refs[:-3])
    send_sems, recv_sems, own_sems = scratch_refs[-3:]
    n_f, half, rows = sizes.n_f, sizes.half, sizes.rows
    width, w_rows, d_rows, own_ff = sizes.width, sizes.w_rows, sizes.d_rows, sizes.own_ff
    part, out_part = sizes.part, sizes.w_rows // CTX
    head = sizes.head

    c = lax.axis_index("ctx")
    f = lax.axis_index("fsdp")
    side = c // 2
    core = c % 2
    place = f // 2
    par = f % 2
    sib = side * 2 + 1 - core
    opp = (1 - side) * 2 + core
    diag = (1 - side) * 2 + 1 - core

    def ctx_dev(index):
        return {"ctx": index, "fsdp": f}

    def f_dev(index):
        return {"ctx": c, "fsdp": index}

    partner = 2 * place + 1 - par

    def other_place(step):
        return lax.rem(place + step, half)

    links = Links(send_sems, recv_sems)

    barrier = pltpu.get_barrier_semaphore()
    for step in range(1, CTX):
        pl.semaphore_signal(
            barrier, inc=1, device_id=ctx_dev(lax.rem(c + step, CTX)), device_id_type=MESH
        )
    for step in range(1, n_f):
        pl.semaphore_signal(
            barrier, inc=1, device_id=f_dev(lax.rem(f + step, n_f)), device_id_type=MESH
        )

    own_copies, leaving = [], []

    def fetch(src, dst):
        made = pltpu.make_async_copy(src, dst, own_sems.at[len(own_copies)])
        own_copies.append(made)
        made.start()
        return made

    def keep(src, dst):
        made = pltpu.make_async_copy(src, dst, own_sems.at[len(own_copies)])
        own_copies.append(made)
        made.start()
        leaving.append(made)

    first_fetches = []
    for third in range(3):
        cols = pl.ds(pl.multiple_of(third * width + c * LANES, LANES), LANES)
        first_fetches.append(
            fetch(wqkv_in.at[:, cols], s.wq.at[f, :, third * LANES : (third + 1) * LANES])
        )
    first_fetches.append(fetch(tok_in, s.tok.at[c]))
    own_block = pl.ds(pl.multiple_of(c * LANES, LANES), LANES)
    later_fetches = [
        fetch(wdown_in.at[pl.ds(pl.multiple_of(c * part, 8), part), :], s.wd.at[f]),
        fetch(wout_in.at[:, own_block], s.wo.at[c, f]),
        fetch(dy_in, s.dy.at[c]),
    ]
    small_in = (vec_in0, vec_in1, vec_in2, vec_in3, vec_in4)
    small_fetches = [fetch(ref, s.ones[at]) for at, ref in enumerate(small_in)]
    small_fetches.append(fetch(bias_in_in, s.bias))
    table_fetches = [fetch(seg_in, s.seg), fetch(table_in, s.table), fetch(rel_in, s.rel)]
    hidden_fetch = fetch(win_in, s.win)
    for made in small_fetches:
        made.wait()
    for at in range(len(small_in)):
        s.vec[f, at : at + 1, 0:w_rows] = s.ones[at][...].astype(F32)
    for at in range(s.bias.shape[0]):
        size = s.bias.shape[1]
        s.vec[f, 5:6, at * size : (at + 1) * size] = s.bias[at : at + 1, :].astype(F32)
    hidden_fetch.wait()
    for at in range(CTX):

        @pl.when(c == at)
        def pick_hidden(at=at):
            starts = [index * d_rows + at * part for index in range(n_f)]
            s.wi[f] = jnp.concatenate([s.win[:, low : low + part] for low in starts], axis=1)

    for made in first_fetches + table_fetches:
        made.wait()

    pl.semaphore_wait(barrier, CTX - 1 + n_f - 1)

    peers = [f_dev(lax.rem(f + step, n_f)) for step in range(1, n_f)]
    far = [2 * other_place(step) + par for step in range(1, half)]
    others = [ctx_dev(lax.rem(c + step, CTX)) for step in range(1, CTX)]

    def to_peers(buf, first):
        piece = buf.at[f]
        links.send_all([(piece, piece)] * (n_f - 1), first, peers, buf.at[0 : n_f - 1])

    def from_peers(buf, first):
        links.wait(buf.at[0 : n_f - 1], first, peers[0])

    def to_group(buf, first):
        piece = buf.at[c]
        links.send_all([(piece, piece)] * (CTX - 1), first, others, buf.at[0 : CTX - 1])

    def from_group(buf, first):
        links.wait(buf.at[0 : CTX - 1], first, others[0])

    def spread(buf, first):
        piece = buf.at[f]
        links.send_all(
            [(piece, piece)] * (half - 1),
            first[0] + place,
            [f_dev(to) for to in far],
            buf.at[0 : half - 1],
        )
        links.send(piece, piece, first[1], f_dev(partner))

    def pass_on(buf, first):
        pairs = []
        for step in range(1, half):
            src = far[step - 1]
            links.wait(buf.at[src], first[0] + src // 2, f_dev(src))
            links.send(buf.at[src], buf.at[src], first[1], f_dev(partner))

    def settle(buf, first):
        links.wait(buf.at[0:half], first[1], f_dev(partner))

    to_peers(s.vec, sem.vec)
    spread(s.wq, sem.wq)
    for to in (sib, opp):
        links.send(s.tok.at[c], s.tok.at[c], sem.tok + c, ctx_dev(to))
    for made in later_fetches:
        made.wait()
    own_out = s.wo.at[c]
    to_peers(own_out, sem.wo[0])
    spread(s.wi, sem.wi)
    spread(s.wd, sem.wd)

    ids = lax.broadcasted_iota(jnp.int32, (sizes.buckets, sizes.group), 0)
    onehot = (ids == s.table[...]).astype(BF16)
    s.hot[...] = onehot.astype(F32)
    s.bvec[...] = mm(s.rel[...], onehot)
    for h in range(2):
        row = s.bvec[pl.ds(2 * c + h, 1), :]
        for delta in range(CTX):
            now = row[:, delta * rows : (delta + 1) * rows]
            before = row[:, (delta - 1) * rows : delta * rows] if delta else now
            wide = jnp.broadcast_to(jnp.concatenate([now, before], axis=1), (rows, 2 * rows))
            turned = pltpu.roll(wide, 0, 1, stride=1, stride_axis=0)
            s.tile[h, delta] = turned[:, :rows]
    seg_f = s.seg[...].astype(F32)
    for at in range(CTX):
        piece = jnp.broadcast_to(seg_f[:, at * rows : (at + 1) * rows], (rows, rows))
        s.segk[at] = jnp.transpose(piece)
    key_pos = lax.broadcasted_iota(jnp.int32, (rows, rows), 0)
    query_pos = lax.broadcasted_iota(jnp.int32, (rows, rows), 1)
    for q_at in range(CTX):
        seg_q = jnp.broadcast_to(seg_f[:, q_at * rows : (q_at + 1) * rows], (rows, rows))
        for k_at in range(q_at + 1):
            seg_k = s.segk[k_at]
            allowed = (seg_k == 0.0) | (seg_k == seg_q)
            if q_at == k_at:
                allowed = allowed & (key_pos <= query_pos)
            for h in range(2):
                block = q_at * (q_at + 1) // 2 + k_at
                s.bm[h, block] = jnp.where(allowed, s.tile[h, q_at - k_at], masked_low)

    from_peers(s.vec, sem.vec)

    def joined(pieces, count, size):
        total = count * size
        spot = lax.broadcasted_iota(jnp.int32, (size, total), 1) % size
        which = lax.broadcasted_iota(jnp.int32, (size, total), 0)
        spreader = (spot == which).astype(BF16)
        flat = mm(pieces.astype(BF16), spreader)
        owner = lax.broadcasted_iota(jnp.int32, (count, total), 1) // size
        mine = owner == lax.broadcasted_iota(jnp.int32, (count, total), 0)
        return jnp.sum(jnp.where(mine, flat, 0.0), axis=0, keepdims=True)

    for at in range(5):
        s.vrow[at : at + 1, :] = joined(s.vec[:, at, 0:w_rows], n_f, w_rows)
    for at in range(CTX):

        @pl.when(c == at)
        def pick_bias(at=at):
            s.vrow[5:6, :] = joined(s.vec[:, 5, at * part : (at + 1) * part], n_f, part)

    gain_one, shift_one = s.vrow[0:1, :], s.vrow[1:2, :]
    gain_two, shift_two = s.vrow[2:3, :], s.vrow[3:4, :]
    bias_down_row, bias_in_row = s.vrow[4:5, :], s.vrow[5:6, :]

    step_rows = 64

    def row_loop(body, count=rows):
        def run(at, carried):
            body(pl.ds(pl.multiple_of(at * step_rows, step_rows), step_rows))
            return carried

        lax.fori_loop(0, count // step_rows, run, 0)

    def first_norm(chunk):
        def body(part):
            hat, scale = norm_stats(s.tok[chunk, part, :].astype(F32))
            s.fn[chunk, part, :] = (hat * gain_one + shift_one).astype(BF16)

        row_loop(body)

    def whole(buf, count, size, kept):
        if size % 16 == 0:
            return buf[...].reshape(count * size, buf.shape[2])
        for at in range(count):
            kept[at * size : (at + 1) * size, :] = buf[at]
        return kept[...]

    head_rows = lax.broadcasted_iota(jnp.int32, (LANES, rows), 0) // head

    def project(chunk):
        weights = whole(s.wq, n_f, w_rows, s.flat_wq)
        made = mm(s.fn[chunk], weights)
        queries = made[:, 0:LANES].astype(BF16).astype(F32) * (head ** -0.5)
        keys = made[:, LANES : 2 * LANES]
        values = made[:, 2 * LANES : 3 * LANES]
        s.k[chunk] = keys.astype(BF16)
        s.v[chunk] = values.astype(BF16)
        s.kt[chunk] = jnp.transpose(keys).astype(BF16)
        s.vt[chunk] = jnp.transpose(values).astype(BF16)
        turned = jnp.transpose(queries)
        for h in range(2):
            kept = jnp.where(head_rows == h, turned, 0.0)
            s.qt[h, chunk] = kept.astype(BF16)
            s.q[h, chunk] = jnp.transpose(kept).astype(BF16)

    first_norm(c)
    pass_on(s.wq, sem.wq)
    links.wait(s.tok.at[sib], sem.tok + sib, ctx_dev(sib))
    first_norm(sib)
    links.wait(s.tok.at[opp], sem.tok + opp, ctx_dev(opp))
    links.send(s.tok.at[opp], s.tok.at[opp], sem.tok + opp, ctx_dev(sib))
    first_norm(opp)

    for to in (sib, opp):
        links.send(s.dy.at[c], s.dy.at[c], sem.dy + c, ctx_dev(to))

    def share_out(to, block):
        links.send(s.wo.at[block], s.wo.at[block], sem.wo[1] + block, ctx_dev(to))

    def wait_out(block, via):
        links.wait(s.wo.at[block], sem.wo[1] + block, ctx_dev(via))

    settle(s.wq, sem.wq)
    project(c)
    project(sib)
    project(opp)
    links.wait(s.tok.at[diag], sem.tok + diag, ctx_dev(sib))
    first_norm(diag)
    project(diag)
    from_peers(own_out, sem.wo[0])
    share_out(sib, c)
    share_out(opp, c)

    def attend(chunk):
        first_block = chunk * (chunk + 1) // 2

        def score_pass(k_at, tops):
            keys = s.k[k_at]
            grown = []
            for h in range(2):
                scores = mm(keys, s.qt[h, chunk]) + s.bm[h, first_block + k_at]
                s.sc[h, k_at] = scores
                grown.append(jnp.maximum(tops[h], jnp.max(scores, axis=0, keepdims=True)))
            return tuple(grown)

        low = jnp.full((1, rows), masked_low, F32)
        tops = lax.fori_loop(0, chunk + 1, score_pass, (low, low))
        s.acc[...] = jnp.zeros((LANES, rows), F32)

        def value_pass(k_at, sums):
            grown = []
            for h in range(2):
                weights = jnp.exp(s.sc[h, k_at] - tops[h])
                grown.append(sums[h] + jnp.sum(weights, axis=0, keepdims=True))
                rounded = weights.astype(BF16)
                s.e[h, first_block + k_at] = rounded
                part = slice(h * head, (h + 1) * head)
                s.acc[part, :] += mm(s.vt[k_at, part, :], rounded)
            return tuple(grown)

        none = jnp.zeros((1, rows), F32)
        sums = lax.fori_loop(0, chunk + 1, value_pass, (none, none))
        for h in range(2):
            part = slice(h * head, (h + 1) * head)
            inverse = 1.0 / sums[h]
            s.linv[chunk, h : h + 1, :] = inverse
            s.att_t[chunk, part, :] = s.acc[part, :] * inverse
        s.att[c, chunk] = jnp.transpose(s.att_t[chunk]).astype(BF16)

    def att_slot(owner, chunk):
        return owner * CTX + chunk

    def send_att(chunk):
        piece = s.att.at[c, chunk]
        for to in (sib, opp):
            links.send(piece, piece, sem.att + att_slot(c, chunk), ctx_dev(to))

    def wait_att(owner, chunk, via):
        links.wait(s.att.at[owner, chunk], sem.att + att_slot(owner, chunk), ctx_dev(via))

    def pass_att(chunk):
        wait_att(opp, chunk, opp)
        piece = s.att.at[opp, chunk]
        links.send(piece, piece, sem.att + att_slot(opp, chunk), ctx_dev(sib))

    mine = [lax.rem(2 * side + step, CTX) for step in range(CTX)]
    theirs = [lax.rem(2 * (1 - side) + step, CTX) for step in range(CTX)]
    attend(mine[0])
    send_att(mine[0])
    attend(mine[1])
    send_att(mine[1])
    pass_on(s.wi, sem.wi)
    pass_att(theirs[0])
    wait_out(opp, opp)
    share_out(sib, opp)
    attend(mine[2])
    send_att(mine[2])
    pass_att(theirs[1])
    links.wait(s.dy.at[opp], sem.dy + opp, ctx_dev(opp))
    links.send(s.dy.at[opp], s.dy.at[opp], sem.dy + opp, ctx_dev(sib))
    attend(mine[3])
    send_att(mine[3])
    pass_on(s.wd, sem.wd)

    wait_out(sib, sib)
    wait_out(diag, sib)
    for block in range(CTX):
        cols = slice(block * LANES, (block + 1) * LANES)
        if w_rows % 16 == 0:
            s.wo_flat[:, cols] = s.wo[block].reshape(width, LANES)
        else:
            for at in range(n_f):
                s.wo_flat[at * w_rows : (at + 1) * w_rows, cols] = s.wo[block, at]

    def gather_att(chunk):
        wait_att(sib, chunk, sib)
        wait_att(diag, chunk, sib)

    def feed(chunk):
        gather_att(chunk)
        mixed = jnp.zeros((rows, width), F32)
        for owner in range(CTX):
            mixed += mm(
                s.att[owner, chunk], s.wo_flat[owner * LANES : (owner + 1) * LANES, :]
            )
        s.mid[...] = mixed + s.tok[chunk].astype(F32)

        def normed(rng):
            hat, scale = norm_stats(s.mid[rng, :])
            s.sn[chunk, rng, :] = (hat * gain_two + shift_two).astype(BF16)

        row_loop(normed)
        s.inner[chunk] = mm(s.sn[chunk], whole(s.wi, n_f, w_rows, s.flat_wi))

    def feed_back(chunk):
        w_down = whole(s.wd, n_f, part, s.flat_wd)
        s.dact[...] = mm(s.dy[chunk], w_down, 1, 1)

        def gelu(rng):
            inner = s.inner[chunk, rng, :] + bias_in_row
            phi = 0.5 + 0.5 * lax.erf(inner * (2.0 ** -0.5))
            slope = phi + inner * (jnp.exp(-0.5 * inner * inner) * (1.0 / math.sqrt(2.0 * math.pi)))
            s.actv[chunk, rng, :] = (inner * phi).astype(BF16)
            s.din[chunk, rng, :] = (s.dact[rng, :] * slope).astype(BF16)

        row_loop(gelu)
        return mm(s.din[chunk], whole(s.wi, n_f, w_rows, s.flat_wi), 1, 1)

    def scatter_first(group, first, part):
        group[0][...] = part.astype(BF16)
        links.send(group[0], group[1], first[0], ctx_dev(sib))

    def scatter_second(group, first, part):
        links.wait(group[1], first[0], ctx_dev(sib))
        group[2][...] = (part + group[1][...].astype(F32)).astype(BF16)
        links.send(group[2], group[3], first[1], ctx_dev(opp))

    def scatter_third(group, first, part):
        group[4][...] = part.astype(BF16)
        links.send(group[4], group[5], first[2], ctx_dev(sib))

    def scatter_wait(group, first):
        links.wait(group[5], first[2], ctx_dev(sib))
        links.wait(group[3], first[1], ctx_dev(opp))

    def scatter_sum(group, part):
        return group[3][part, :].astype(F32) + group[5][part, :].astype(F32)

    settle(s.wi, sem.wi)
    feed(diag)
    pass_att(theirs[2])
    feed(opp)
    pass_att(theirs[3])
    feed(sib)
    feed(c)
    settle(s.wd, sem.wd)
    links.wait(s.dy.at[diag], sem.dy + diag, ctx_dev(sib))
    scatter_first(s.rs_s, sem.rs_s, feed_back(diag))
    scatter_second(s.rs_s, sem.rs_s, feed_back(opp))
    links.wait(s.dy.at[sib], sem.dy + sib, ctx_dev(sib))
    scatter_third(s.rs_s, sem.rs_s, feed_back(sib))
    s.dsec[...] = feed_back(c)

    def even_pieces(group, left, right, cols, size):
        for at in range(left.shape[2] // LANES):
            lhs = left[:, :, at * LANES : (at + 1) * LANES].reshape(CTX * rows, LANES)
            made = mm(lhs, right[...].reshape(CTX * rows, cols), 0, 0).astype(BF16)
            for piece in range(LANES // size):
                to = at * (LANES // size) + piece
                group[0][to % 2, to // 2] = made[piece * size : (piece + 1) * size, :]

    def grad_pair(group, first):
        links.send(group[0].at[1 - par], group[1], first[0], f_dev(partner))

    def grad_even_second(group, first):
        links.wait(group[1], first[0], f_dev(partner))
        group[2][...] = (
            group[0][par].astype(F32) + group[1][...].astype(F32)
        ).astype(BF16)
        pairs = [(group[2].at[to // 2], group[3].at[place]) for to in far]
        links.send_all(pairs, first[1], [f_dev(to) for to in far], group[3].at[0 : half - 1])

    def grad_even_third(group, first):
        links.wait(group[3].at[0 : half - 1], first[1], f_dev(far[0]))
        total = group[2][place].astype(F32)
        for src in far:
            total += group[3][src // 2].astype(F32)
        group[4][c] = total.astype(BF16)
        to_group(group[4], first[2])

    def grad_direct(group, first):
        pairs = [
            (group[0].at[lax.rem(f + step, n_f)], group[1].at[f]) for step in range(1, n_f)
        ]
        links.send_all(pairs, first[0], peers, group[1].at[0 : n_f - 1])

    def grad_direct_sum(group, first):
        from_peers(group[1], first[0])
        total = group[0][f].astype(F32)
        for step in range(1, n_f):
            total += group[1][lax.rem(f + step, n_f)].astype(F32)
        group[2][c] = total.astype(BF16)
        to_group(group[2], first[1])

    even_pieces(s.gd, s.actv, s.dy, width, part)
    grad_pair(s.gd, sem.gd)
    even_pieces(s.gi, s.sn, s.din, own_ff, w_rows)
    grad_pair(s.gi, sem.gi)
    w_down = whole(s.wd, n_f, part, s.flat_wd)
    scatter_first(s.rs_o, sem.rs_o, mm(s.actv[diag], w_down))
    scatter_third(s.rs_o, sem.rs_o, mm(s.actv[sib], w_down))

    scatter_wait(s.rs_s, sem.rs_s)
    s.vg[...] = jnp.zeros_like(s.vg)

    def second_back(rng):
        hat, scale = norm_stats(s.mid[rng, :])
        d_second = s.dsec[rng, :] + scatter_sum(s.rs_s, rng)
        d_result = s.dy[c, rng, :].astype(F32)
        d_middle = d_result + norm_back(d_second, gain_two, hat, scale)
        s.dmid[rng, :] = d_middle
        s.dmx[rng, :] = d_middle.astype(BF16)
        s.vg[2:3, :] += jnp.sum(d_second * hat, axis=0, keepdims=True)
        s.vg[3:4, :] += jnp.sum(d_second, axis=0, keepdims=True)
        s.vg[4:5, :] += jnp.sum(d_result, axis=0, keepdims=True)

    row_loop(second_back)
    d_att = mm(s.wo_flat[...], s.dmx[...], 1, 1)
    s.dat_out[...] = d_att.astype(BF16).reshape(CTX, LANES, rows)
    for to in (opp, diag, sib):
        links.send(s.dat_out.at[to], s.dat.at[c], sem.dat + c, ctx_dev(to))
    s.dat[c] = s.dat_out[c]
    for owner in range(CTX):
        made = mm(s.att[owner, c], s.dmx[...], 0, 0).astype(BF16)
        for piece in range(LANES // w_rows):
            at = owner * (LANES // w_rows) + piece
            for part_at in range(CTX):
                low = piece * w_rows + part_at * out_part
                s.go_own[part_at % 2, part_at // 2, at] = made[low : low + out_part, :]
    links.send(s.go_own.at[1 - core], s.go_core, sem.go_core, ctx_dev(sib))
    grad_even_second(s.gd, sem.gd)
    links.wait(s.go_core, sem.go_core, ctx_dev(sib))
    s.go_two[...] = (
        s.go_own[core].astype(F32) + s.go_core[...].astype(F32)
    ).astype(BF16)
    links.send(s.go_two.at[1 - side], s.go_side, sem.go_side, ctx_dev(opp))
    scatter_second(s.rs_o, sem.rs_o, mm(s.actv[opp], w_down))
    s.outp[...] = s.mid[...] + mm(s.actv[c], w_down) + bias_down_row
    for at in range(CTX):

        def bias_rows(rng, at=at):
            s.vg[5:6, :] += jnp.sum(s.din[at, rng, :].astype(F32), axis=0, keepdims=True)

        row_loop(bias_rows)

    for src in (sib, opp, diag):
        links.wait(s.dat.at[src], sem.dat + src, ctx_dev(src))
    for at in range(CTX):
        got = s.dat[at].astype(F32)
        for h in range(2):
            part = slice(h * head, (h + 1) * head)
            scaled = (got * s.linv[at, h : h + 1, :]).astype(BF16)
            kept = jnp.where(head_rows == h, scaled.astype(F32), 0.0)
            s.dat_t[h, at] = kept.astype(BF16)
            s.dat_n[h, at] = jnp.transpose(kept).astype(BF16)
            s.delta[at, h : h + 1, :] = jnp.sum(
                kept[part, :] * s.att_t[at, part, :], axis=0, keepdims=True
            )
        s.dqt[at] = jnp.zeros((LANES, rows), F32)
        s.dk[at] = jnp.zeros((rows, LANES), F32)
    s.dbm[...] = jnp.zeros_like(s.dbm)

    def block_pair(q_at, k_at):
        block = q_at * (q_at + 1) // 2 + k_at
        values = s.v[k_at]
        for h in range(2):
            lanes = slice(h * head, (h + 1) * head)
            d_probs = mm(values, s.dat_t[h, q_at])
            rounded = s.e[h, block]
            d_scores = rounded.astype(F32) * (d_probs - s.delta[q_at, h : h + 1, :])
            s.dbm[h, q_at - k_at] += d_scores
            low = d_scores.astype(BF16)
            s.dk[k_at] += mm(low, s.q[h, q_at])
            s.dqt[q_at, lanes, :] += mm(s.kt[k_at, lanes, :], low)

    def query_row(upper):
        def run(lower, carried):
            shift = side * (CTX - 1 - upper - lower)
            block_pair(upper + shift, lower + shift)
            return carried

        lax.fori_loop(0, upper + 1, run, 0)

    def pack(chunk):
        s.dp[chunk, :, 0:LANES] = (jnp.transpose(s.dqt[chunk]) * (head ** -0.5)).astype(BF16)
        s.dp[chunk, :, LANES : 2 * LANES] = s.dk[chunk].astype(BF16)

    w_qkv = whole(s.wq, n_f, w_rows, s.flat_wq)

    def back_first(chunk):
        s.dsec[...] = mm(s.dp[chunk], w_qkv, 1, 1)

        def add_rows(rng):
            part_rows = s.dsec[rng, :]
            s.vg[0:1, :] += jnp.sum(s.fn[chunk, rng, :].astype(F32) * part_rows, axis=0, keepdims=True)
            s.vg[1:2, :] += jnp.sum(part_rows, axis=0, keepdims=True)

        return add_rows

    def value_grads(k_at):
        made = jnp.zeros((rows, LANES), F32)
        for q_at in range(k_at, CTX):
            block = q_at * (q_at + 1) // 2 + k_at
            for h in range(2):
                made += mm(s.e[h, block], s.dat_n[h, q_at])
        s.dp[k_at, :, 2 * LANES : 3 * LANES] = made.astype(BF16)

    def qkv_pieces(group, cols):
        for at in range(width // LANES):
            lhs = s.fn[:, :, at * LANES : (at + 1) * LANES].reshape(CTX * rows, LANES)
            rhs = s.dp[:, :, cols].reshape(CTX * rows, cols.stop - cols.start)
            made = mm(lhs, rhs, 0, 0).astype(BF16)
            for piece in range(LANES // w_rows):
                to = at * (LANES // w_rows) + piece
                group[0][to] = made[piece * w_rows : (piece + 1) * w_rows, :]

    for at in range(CTX):
        value_grads(at)
    qkv_pieces(s.gv, slice(2 * LANES, 3 * LANES))
    grad_direct(s.gv, sem.gv)
    query_row(3)
    grad_even_second(s.gi, sem.gi)
    links.wait(s.go_side, sem.go_side, ctx_dev(opp))
    s.go[0][...] = (s.go_two[side].astype(F32) + s.go_side[...].astype(F32)).astype(BF16)
    grad_direct(s.go, sem.go)
    query_row(2)
    pack(diag)
    pack(opp)
    sums = back_first(diag)
    scatter_first(s.rs_f, sem.rs_f, s.dsec[...])
    row_loop(sums)
    sums = back_first(opp)
    scatter_second(s.rs_f, sem.rs_f, s.dsec[...])
    row_loop(sums)
    query_row(1)
    query_row(0)
    pack(sib)
    pack(c)
    qkv_pieces(s.gq, slice(0, 2 * LANES))
    grad_direct(s.gq, sem.gq)
    grad_direct_sum(s.gv, sem.gv)
    sums = back_first(sib)
    scatter_third(s.rs_f, sem.rs_f, s.dsec[...])
    row_loop(sums)
    sums = back_first(c)
    row_loop(sums)

    for h in range(2):
        pieces = []
        for delta in range(CTX):
            block = s.dbm[h, delta]
            wide = jnp.concatenate([block, jnp.zeros((rows, rows), F32)], axis=1)
            count = rows
            while count > 1:
                count //= 2
                turned = pltpu.roll(wide[count : 2 * count, :], 2 * rows - count, 1)
                wide = wide[0:count, :] + turned
            pieces.append(wide)
        total = []
        for delta in range(CTX):
            here = pieces[delta][:, 0:rows]
            if delta + 1 < CTX:
                here = here + pieces[delta + 1][:, rows : 2 * rows]
            total.append(here)
        dist = jnp.concatenate(total, axis=1)
        bucket_sums = lax.dot_general(
            jnp.broadcast_to(dist, (8, sizes.group)),
            s.hot[...],
            (((1,), (1,)), ((), ())),
            preferred_element_type=F32,
            precision=lax.Precision.HIGHEST,
        )
        s.vg[6 + h : 7 + h, 0 : sizes.buckets] = bucket_sums[0:1, :]

    s.vg[0:1, :] = (s.vg[0:1, :] - shift_one * s.vg[1:2, :]) / gain_one
    for to in range(n_f):
        s.vgp[to, :, 0:w_rows] = s.vg[:, to * w_rows : (to + 1) * w_rows]
        s.vgp[to, 6:8, 0 : sizes.buckets] = s.vg[6:8, 0 : sizes.buckets]
    pairs = [(s.vgp.at[lax.rem(f + step, n_f)], s.vgf.at[f]) for step in range(1, n_f)]
    links.send_all(pairs, sem.vgf, peers, s.vgf.at[0 : n_f - 1])

    grad_even_third(s.gd, sem.gd)
    scatter_wait(s.rs_f, sem.rs_f)

    def first_back(rng):
        hat, scale = norm_stats(s.tok[c, rng, :].astype(F32))
        d_first = s.dsec[rng, :] + scatter_sum(s.rs_f, rng)
        d_x = s.dmid[rng, :] + norm_back(d_first, gain_one, hat, scale)
        s.dx[rng, :] = d_x.astype(BF16)

    row_loop(first_back)
    keep(s.dx, dx_ref)
    grad_direct_sum(s.gq, sem.gq)
    from_peers(s.vgf, sem.vgf)
    total = s.vgp[f]
    for step in range(1, n_f):
        total += s.vgf[lax.rem(f + step, n_f)]
    s.vgc[c] = total
    to_group(s.vgc, sem.vgc)
    grad_direct_sum(s.go, sem.go)
    grad_even_third(s.gi, sem.gi)

    scatter_wait(s.rs_o, sem.rs_o)
    s.out[...] = (
        s.outp[...] + s.rs_o[3][...].astype(F32) + s.rs_o[5][...].astype(F32)
    ).astype(BF16)
    keep(s.out, out_ref)
    from_group(s.gd[4], sem.gd[2])
    keep(s.gd[4], gdown_ref)
    from_group(s.gv[2], sem.gv[1])
    keep(s.gv[2], gv_ref)
    from_group(s.gq[2], sem.gq[1])
    keep(s.gq[2], gqk_ref)
    from_group(s.vgc, sem.vgc)
    keep(s.vgc, small_ref)
    from_group(s.go[2], sem.go[1])
    keep(s.go[2], gout_ref)
    from_group(s.gi[4], sem.gi[2])
    keep(s.gi[4], gin_ref)
    links.drain()
    for made in leaving:
        made.wait()


def finish_kernel(
    sizes,
    out_in,
    dx_in,
    gqk_in,
    gv_in,
    gout_in,
    gin_in,
    gdown_in,
    small_in,
    out_ref,
    dx_ref,
    gqkv_ref,
    gout_ref,
    gin_ref,
    gdown_ref,
    gg1_ref,
    gs1_ref,
    gg2_ref,
    gs2_ref,
    gbi_ref,
    gbd_ref,
    grel_ref,
    gqkv,
    gout,
    gin,
    gdown,
    gqk_low,
    gv_low,
    gout_low,
    gin_low,
    gdown_low,
    out_low,
    dx_low,
    sems,
):
    made = []

    def start(src, dst):
        copy = pltpu.make_async_copy(src, dst, sems.at[len(made)])
        copy.start()
        made.append(copy)
        return copy

    loads = [
        start(gdown_in, gdown_low),
        start(gin_in, gin_low),
        start(gqk_in, gqk_low),
        start(gout_in, gout_low),
    ]
    loads += [start(out_in, out_low), start(dx_in, dx_low), start(gv_in, gv_low)]
    width, own_ff = sizes.width, sizes.own_ff
    loads[0].wait()
    for at in range(CTX):
        gdown[at * sizes.part : (at + 1) * sizes.part, :] = gdown_low[at].astype(F32)
    stores = [start(gdown, gdown_ref)]
    loads[1].wait()
    part = sizes.part
    for index in range(sizes.n_f):
        lanes = slice(index * part, (index + 1) * part)
        joined = jnp.concatenate([gin_low[at, :, lanes].astype(F32) for at in range(CTX)], axis=1)
        gin[:, index * CTX * part : (index + 1) * CTX * part] = joined
    stores.append(start(gin, gin_ref))
    loads[2].wait()
    loads[6].wait()
    for at in range(CTX):
        for third in range(3):
            low = third * width + at * LANES
            if third == 2:
                got = gv_low[at]
            else:
                got = gqk_low[at, :, third * LANES : (third + 1) * LANES]
            gqkv[:, low : low + LANES] = got.astype(F32)
    stores.append(start(gqkv, gqkv_ref))
    loads[3].wait()
    out_part = sizes.w_rows // CTX
    for at in range(CTX):
        gout[at * out_part : (at + 1) * out_part, :] = gout_low[at].astype(F32)
    stores.append(start(gout, gout_ref))
    loads[4].wait()
    stores.append(start(out_low, out_ref))
    loads[5].wait()
    stores.append(start(dx_low, dx_ref))
    total = jnp.sum(small_in[...], axis=0)
    for at, ref in enumerate((gg1_ref, gs1_ref, gg2_ref, gs2_ref, gbd_ref)):
        ref[...] = total[at : at + 1, 0 : sizes.w_rows]
    size = gbi_ref.shape[1]
    hidden = jnp.concatenate([small_in[at, 5:6, 0 : sizes.part] for at in range(CTX)], axis=1)
    for at in range(gbi_ref.shape[0]):
        gbi_ref[at : at + 1, :] = hidden[:, at * size : (at + 1) * size]
    for at in range(CTX):
        grel_ref[2 * at : 2 * at + 2, :] = small_in[at, 6:8, 0 : sizes.buckets]
    for copy in stores:
        copy.wait()


def scratch_spec(z):
    rows, width, group = z.rows, z.width, z.group
    blocks = CTX * (CTX + 1) // 2
    act = (CTX, rows, width)
    hidden = (CTX, rows, z.own_ff)
    tall = (CTX, rows, LANES)
    wide = (CTX, LANES, rows)
    squares = (2, CTX, rows, rows)

    def scatter():
        flat = ((rows, width), BF16)
        landing = ((rows, width), BF16, 1)
        return [flat, landing, flat, landing, flat, landing]

    def even(size, cols):
        part = (z.half, size, cols)
        return [
            ((2,) + part, BF16),
            (part, BF16, 1),
            (part, BF16),
            (part, BF16, 1),
            ((CTX, size, cols), BF16, 1),
        ]

    def direct(size, cols):
        whole = (z.n_f, size, cols)
        return [(whole, BF16), (whole, BF16, 1), ((CTX, size, cols), BF16, 1)]

    out_part = z.w_rows // CTX
    out_rows = (z.n_f, out_part, width)
    spec = dict(
        tok=(act, BF16, CTX),
        dy=(act, BF16, CTX),
        fn=(act, BF16),
        wq=((z.n_f, z.w_rows, 3 * LANES), BF16, z.half, 1),
        wo=((CTX, z.n_f, z.w_rows, LANES), BF16, 1, CTX),
        wo_flat=((width, width), BF16),
        wi=((z.n_f, z.w_rows, z.own_ff), BF16, z.half, 1),
        wd=((z.n_f, z.part, width), BF16, z.half, 1),
        vec=((z.n_f, 8, max(z.d_rows, LANES)), F32, 1),
        ones=[((1, z.w_rows), BF16)] * 5,
        bias=((max(1, z.d_rows // LANES), min(LANES, z.d_rows)), BF16),
        seg=((1, group), jnp.int32),
        table=((1, group), jnp.int32),
        rel=((z.heads, z.buckets), BF16),
        win=((z.w_rows, z.ff), BF16),
        out=((rows, width), BF16),
        dx=((rows, width), BF16),
        vrow=((8, width), F32),
        hot=((z.buckets, group), F32),
        bvec=((8, group), F32),
        tile=(squares, F32),
        segk=((CTX, rows, rows), F32),
        bm=((2, blocks, rows, rows), F32),
        k=(tall, BF16),
        v=(tall, BF16),
        kt=(wide, BF16),
        vt=(wide, BF16),
        qt=((2,) + wide, BF16),
        q=((2,) + tall, BF16),
        sc=(squares, F32),
        e=((2, blocks, rows, rows), BF16),
        acc=((LANES, rows), F32),
        linv=((CTX, 8, rows), F32),
        att_t=(wide, F32),
        att=((CTX,) + tall, BF16, CTX * CTX),
        mid=((rows, width), F32),
        sn=(act, BF16),
        inner=((CTX, rows, z.own_ff), F32),
        dact=((rows, z.own_ff), F32),
        actv=(hidden, BF16),
        din=(hidden, BF16),
        dsec=((rows, width), F32),
        outp=((rows, width), F32),
        dmid=((rows, width), F32),
        dmx=((rows, width), BF16),
        dat_out=(wide, BF16),
        dat=(wide, BF16, CTX),
        dat_t=((2,) + wide, BF16),
        dat_n=((2,) + tall, BF16),
        delta=((CTX, 8, rows), F32),
        dqt=(wide, F32),
        dbm=(squares, F32),
        dk=(tall, F32),
        dp=((CTX, rows, 3 * LANES), BF16),
        vg=((8, width), F32),
        vgp=((z.n_f, 8, LANES), F32),
        vgf=((z.n_f, 8, LANES), F32, 1),
        vgc=((CTX, 8, LANES), F32, 1),
        rs_s=scatter(),
        rs_o=scatter(),
        rs_f=scatter(),
        gq=direct(z.w_rows, 2 * LANES),
        gv=direct(z.w_rows, LANES),
        gi=even(z.w_rows, z.own_ff),
        gd=even(z.part, width),
        go=direct(out_part, width),
        go_own=((2, 2) + out_rows, BF16),
        go_core=((2,) + out_rows, BF16, 1),
        go_two=((2,) + out_rows, BF16),
        go_side=(out_rows, BF16, 1),
    )
    if z.w_rows % 16:
        spec.update(
            flat_wq=((width, 3 * LANES), BF16),
            flat_wi=((width, z.own_ff), BF16),
        )
    else:
        spec.update(flat_wq=((8, LANES), BF16), flat_wi=((8, LANES), BF16))
    flat_shape = (z.own_ff, width) if z.part % 16 else (8, LANES)
    spec.update(flat_wd=(flat_shape, BF16))
    return spec


def scratch_items(spec):
    for item in spec.values():
        if isinstance(item, list):
            yield from item
        else:
            yield item


def name_scratch(spec, refs):
    refs = iter(refs)
    by_name, first, used = {}, {}, 0
    for name, item in spec.items():
        entries = item if isinstance(item, list) else [item]
        held, starts = [], []
        for entry in entries:
            held.append(next(refs))
            for count in entry[2:]:
                starts.append(used)
                used += count
        by_name[name] = held if isinstance(item, list) else held[0]
        if starts:
            first[name] = starts if isinstance(item, list) or len(starts) > 1 else starts[0]
    return SimpleNamespace(**by_name), SimpleNamespace(**first)


def per_device(
    n_f,
    tokens,
    segment_ids,
    bucket_table,
    w_qkv,
    w_out,
    w_in,
    w_down,
    gain_one,
    shift_one,
    gain_two,
    shift_two,
    bias_in,
    bias_down,
    rel_bias,
    cotangent,
):
    sizes = Sizes(
        n_f,
        tokens.shape[1],
        tokens.shape[2],
        w_in.shape[1],
        segment_ids.shape[1],
        rel_bias.shape[0],
        rel_bias.shape[1],
    )
    rows, width, w_rows, d_rows = sizes.rows, sizes.width, sizes.w_rows, sizes.d_rows
    vmem = pl.BlockSpec(memory_space=pltpu.VMEM)
    far = pl.BlockSpec(memory_space=pltpu.HBM)
    spec = scratch_spec(sizes)
    n_recv = sum(sum(item[2:]) for item in scratch_items(spec))
    bias_shape = (max(1, d_rows // LANES), min(LANES, d_rows))
    shaped = jax.ShapeDtypeStruct
    made = pl.pallas_call(
        functools.partial(layer_kernel, sizes),
        out_shape=[
            shaped((rows, width), BF16),
            shaped((rows, width), BF16),
            shaped((CTX, w_rows, 2 * LANES), BF16),
            shaped((CTX, w_rows, LANES), BF16),
            shaped((CTX, w_rows // CTX, width), BF16),
            shaped((CTX, w_rows, sizes.own_ff), BF16),
            shaped((CTX, sizes.part, width), BF16),
            shaped((CTX, 8, LANES), F32),
        ],
        in_specs=[far] * 15,
        out_specs=[far] * 8,
        scratch_shapes=[pltpu.VMEM(item[0], item[1]) for item in scratch_items(spec)]
        + [
            pltpu.SemaphoreType.DMA((SENDS,)),
            pltpu.SemaphoreType.DMA((n_recv,)),
            pltpu.SemaphoreType.DMA((26,)),
        ],
        compiler_params=pltpu.CompilerParams(
            collective_id=0, has_side_effects=True, vmem_limit_bytes=60 * 1024 * 1024
        ),
        name="layer",
    )(
        tokens[0],
        segment_ids,
        bucket_table[None],
        w_qkv,
        w_out,
        w_in,
        w_down,
        gain_one[None],
        shift_one[None],
        gain_two[None],
        shift_two[None],
        bias_down[None],
        bias_in.reshape(bias_shape),
        jnp.transpose(rel_bias),
        cotangent[0],
    )
    outs = [
        ((rows, width), BF16),
        ((rows, width), BF16),
        ((w_rows, 3 * width), F32),
        ((w_rows, width), F32),
        ((w_rows, sizes.ff), F32),
        ((d_rows, width), F32),
        ((1, w_rows), F32),
        ((1, w_rows), F32),
        ((1, w_rows), F32),
        ((1, w_rows), F32),
        (bias_shape, F32),
        ((1, w_rows), F32),
        ((sizes.heads, sizes.buckets), F32),
    ]
    done = pl.pallas_call(
        functools.partial(finish_kernel, sizes),
        out_shape=[shaped(shape, kind) for shape, kind in outs],
        in_specs=[far] * 7 + [vmem],
        out_specs=[far] * 6 + [vmem] * 7,
        scratch_shapes=[pltpu.VMEM(shape, kind) for shape, kind in outs[2:6]]
        + [pltpu.VMEM(item.shape, item.dtype) for item in made[2:7] + made[0:2]]
        + [pltpu.SemaphoreType.DMA((14,))],
        compiler_params=pltpu.CompilerParams(vmem_limit_bytes=60 * 1024 * 1024),
        name="finish",
    )(*made)
    return (
        done[0][None],
        done[1][None],
        done[2],
        done[3],
        done[4],
        done[5],
        done[6][0],
        done[7][0],
        done[8][0],
        done[9][0],
        done[10].reshape(-1),
        done[11][0],
        jnp.transpose(done[12]),
    )


def solution(mesh):
    by_f, by_both = P("fsdp"), P("fsdp", "ctx", None)
    in_specs = (by_both, by_f, P()) + (by_f,) * 10 + (P(), by_both)
    out_specs = (by_both, by_both) + (by_f,) * 10 + (P(),)
    return jax.shard_map(
        functools.partial(per_device, mesh.shape["fsdp"]),
        mesh=mesh,
        in_specs=in_specs,
        out_specs=out_specs,
        check_vma=False,
    )
```

time: 112 us -> 88.7 us (0.79)
  the two profiles are of different devices: /device:TPU:0 before, /device:TPU:27 now
where the time goes in v2:
time: 88.7 us; the launch traced here: 88.4 us
  Pallas kernels  87.6 us (99%)
    pallas_call x1, Pallas kernels, per_device(): pl.pallas_call(functools.partial(layer_kernel, sizes), out_shape=[shaped(...  83.8 us
    pallas_call x1, Pallas kernels, per_device(): pl.pallas_call(functools.partial(finish_kernel, sizes), out_shape=[shaped...  3.76 us

profile of v2, /device:TPU:27, one launch (start us, length us, event | category | flops | bytes accessed | tf_op | source)
XLA Modules:
  0.0 88.4 jit_solution(16510899981771501426)
XLA Ops:
  0.7 83.8 %layer.1 = (bf16[256,512]{1,0:T(8,128)(2,1)}, bf16[256,512]{1,0:T(8,128)(2,1)}, bf16[4,64,256]{2,1,0:T(8,128)(2,1)}, bf16[4,64,128]{2,1,0:T(8,128)(2,1)}, bf16[4...) custom-call(bf16[256,512]{1,0:T(8,128)(2,1)} %bitcast.19, ...), custom_call_target="tpu_custom_call" | custom-call | tf_op jit(solution)/shard_map/layer/pallas_call | solution.py:1081
  84.5 3.8 %finish.1 = (bf16[256,512]{1,0:T(8,128)(2,1)}, bf16[256,512]{1,0:T(8,128)(2,1)}, f32[64,1536]{1,0:T(8,128)}, f32[64,512]{1,0:T(8,128)}, f32[64,2048]{1,0:T(8,128...) custom-call(bf16[256,512]{1,0:T(8,128)(2,1)} %get-tuple-element.34.o, ...), custom_call_target="tpu_custom_call" | custom-call | tf_op jit(solution)/shard_map/finish/pallas_call | solution.py:1137

commit v3 on v2

--- a/solution.py
+++ b/solution.py
@@ -95,7 +95,7 @@
         self.pending = []
 
 
-SENDS = 96
+SENDS = 128
 
 
 def layer_kernel(
@@ -255,16 +255,13 @@
     def settle(buf, first):
         links.wait(buf.at[0:half], first[1], f_dev(partner))
 
+    for to in (sib, opp):
+        links.send(s.tok.at[c], s.tok.at[c], sem.tok + c, ctx_dev(to))
     to_peers(s.vec, sem.vec)
     spread(s.wq, sem.wq)
-    for to in (sib, opp):
-        links.send(s.tok.at[c], s.tok.at[c], sem.tok + c, ctx_dev(to))
     for made in later_fetches:
         made.wait()
     own_out = s.wo.at[c]
-    to_peers(own_out, sem.wo[0])
-    spread(s.wi, sem.wi)
-    spread(s.wd, sem.wd)
 
     ids = lax.broadcasted_iota(jnp.int32, (sizes.buckets, sizes.group), 0)
     onehot = (ids == s.table[...]).astype(BF16)
@@ -362,6 +359,9 @@
 
     first_norm(c)
     pass_on(s.wq, sem.wq)
+    to_peers(own_out, sem.wo[0])
+    spread(s.wi, sem.wi)
+    spread(s.wd, sem.wd)
     links.wait(s.tok.at[sib], sem.tok + sib, ctx_dev(sib))
     first_norm(sib)
     links.wait(s.tok.at[opp], sem.tok + opp, ctx_dev(opp))
@@ -388,41 +388,31 @@
     share_out(sib, c)
     share_out(opp, c)
 
-    def attend(chunk):
+    def attend_rows(chunk):
         first_block = chunk * (chunk + 1) // 2
-
-        def score_pass(k_at, tops):
-            keys = s.k[k_at]
-            grown = []
-            for h in range(2):
-                scores = mm(keys, s.qt[h, chunk]) + s.bm[h, first_block + k_at]
+        for h in range(2):
+            top = jnp.full((1, rows), masked_low, F32)
+            for k_at in range(chunk + 1):
+                scores = mm(s.k[k_at], s.qt[h, chunk]) + s.bm[h, first_block + k_at]
                 s.sc[h, k_at] = scores
-                grown.append(jnp.maximum(tops[h], jnp.max(scores, axis=0, keepdims=True)))
-            return tuple(grown)
-
-        low = jnp.full((1, rows), masked_low, F32)
-        tops = lax.fori_loop(0, chunk + 1, score_pass, (low, low))
-        s.acc[...] = jnp.zeros((LANES, rows), F32)
-
-        def value_pass(k_at, sums):
-            grown = []
-            for h in range(2):
-                weights = jnp.exp(s.sc[h, k_at] - tops[h])
-                grown.append(sums[h] + jnp.sum(weights, axis=0, keepdims=True))
+                top = jnp.maximum(top, jnp.max(scores, axis=0, keepdims=True))
+            lanes = slice(h * head, (h + 1) * head)
+            total = jnp.zeros((1, rows), F32)
+            mixed = jnp.zeros((head, rows), F32)
+            for k_at in range(chunk + 1):
+                weights = jnp.exp(s.sc[h, k_at] - top)
+                total = total + jnp.sum(weights, axis=0, keepdims=True)
                 rounded = weights.astype(BF16)
                 s.e[h, first_block + k_at] = rounded
-                part = slice(h * head, (h + 1) * head)
-                s.acc[part, :] += mm(s.vt[k_at, part, :], rounded)
-            return tuple(grown)
-
-        none = jnp.zeros((1, rows), F32)
-        sums = lax.fori_loop(0, chunk + 1, value_pass, (none, none))
-        for h in range(2):
-            part = slice(h * head, (h + 1) * head)
-            inverse = 1.0 / sums[h]
+                mixed = mixed + mm(s.vt[k_at, lanes, :], rounded)
+            inverse = 1.0 / total
             s.linv[chunk, h : h + 1, :] = inverse
-            s.att_t[chunk, part, :] = s.acc[part, :] * inverse
+            s.att_t[chunk, lanes, :] = mixed * inverse
         s.att[c, chunk] = jnp.transpose(s.att_t[chunk]).astype(BF16)
+
+    def attend(turn):
+        for which in range(2):
+            pl.when(side == which)(functools.partial(attend_rows, (2 * which + turn) % CTX))
 
     def att_slot(owner, chunk):
         return owner * CTX + chunk
@@ -442,22 +432,22 @@
 
     mine = [lax.rem(2 * side + step, CTX) for step in range(CTX)]
     theirs = [lax.rem(2 * (1 - side) + step, CTX) for step in range(CTX)]
-    attend(mine[0])
+    attend(0)
     send_att(mine[0])
-    attend(mine[1])
+    attend(1)
     send_att(mine[1])
     pass_on(s.wi, sem.wi)
     pass_att(theirs[0])
     wait_out(opp, opp)
     share_out(sib, opp)
-    attend(mine[2])
+    attend(2)
     send_att(mine[2])
+    pass_on(s.wd, sem.wd)
     pass_att(theirs[1])
     links.wait(s.dy.at[opp], sem.dy + opp, ctx_dev(opp))
     links.send(s.dy.at[opp], s.dy.at[opp], sem.dy + opp, ctx_dev(sib))
-    attend(mine[3])
+    attend(3)
     send_att(mine[3])
-    pass_on(s.wd, sem.wd)
 
     wait_out(sib, sib)
     wait_out(diag, sib)
@@ -547,15 +537,22 @@
                 group[0][to % 2, to // 2] = made[piece * size : (piece + 1) * size, :]
 
     def grad_pair(group, first):
-        links.send(group[0].at[1 - par], group[1], first[0], f_dev(partner))
-
-    def grad_even_second(group, first):
-        links.wait(group[1], first[0], f_dev(partner))
-        group[2][...] = (
-            group[0][par].astype(F32) + group[1][...].astype(F32)
-        ).astype(BF16)
-        pairs = [(group[2].at[to // 2], group[3].at[place]) for to in far]
-        links.send_all(pairs, first[1], [f_dev(to) for to in far], group[3].at[0 : half - 1])
+        for to in far:
+            links.send(
+                group[0].at[1 - par, to // 2], group[1].at[to // 2], first[0] + to // 2, f_dev(partner)
+            )
+        links.send(group[0].at[1 - par, place], group[1].at[place], first[0] + place, f_dev(partner))
+
+    def grad_step(group, first, step):
+        at = far[step] // 2 if step < half - 1 else place
+        links.wait(group[1].at[at], first[0] + at, f_dev(partner))
+        group[2][at] = (group[0][par, at].astype(F32) + group[1][at].astype(F32)).astype(BF16)
+        if step < half - 1:
+            links.send(group[2].at[at], group[3].at[place], first[1], f_dev(far[step]))
+
+    def grad_steps(group, first, low=0, high=half):
+        for step in range(low, high):
+            grad_step(group, first, step)
 
     def grad_even_third(group, first):
         links.wait(group[3].at[0 : half - 1], first[1], f_dev(far[0]))
@@ -586,6 +583,7 @@
     w_down = whole(s.wd, n_f, part, s.flat_wd)
     scatter_first(s.rs_o, sem.rs_o, mm(s.actv[diag], w_down))
     scatter_third(s.rs_o, sem.rs_o, mm(s.actv[sib], w_down))
+    grad_steps(s.gd, sem.gd, 0, half // 2)
 
     scatter_wait(s.rs_s, sem.rs_s)
     s.vg[...] = jnp.zeros_like(s.vg)
@@ -615,7 +613,7 @@
                 low = piece * w_rows + part_at * out_part
                 s.go_own[part_at % 2, part_at // 2, at] = made[low : low + out_part, :]
     links.send(s.go_own.at[1 - core], s.go_core, sem.go_core, ctx_dev(sib))
-    grad_even_second(s.gd, sem.gd)
+    grad_steps(s.gd, sem.gd, half // 2, half)
     links.wait(s.go_core, sem.go_core, ctx_dev(sib))
     s.go_two[...] = (
         s.go_own[core].astype(F32) + s.go_core[...].astype(F32)
@@ -629,6 +627,7 @@
             s.vg[5:6, :] += jnp.sum(s.din[at, rng, :].astype(F32), axis=0, keepdims=True)
 
         row_loop(bias_rows)
+    grad_steps(s.gi, sem.gi, 0, half // 2)
 
     for src in (sib, opp, diag):
         links.wait(s.dat.at[src], sem.dat + src, ctx_dev(src))
@@ -699,17 +698,24 @@
             made = mm(lhs, rhs, 0, 0).astype(BF16)
             for piece in range(LANES // w_rows):
                 to = at * (LANES // w_rows) + piece
-                group[0][to] = made[piece * w_rows : (piece + 1) * w_rows, :]
+                got = made[piece * w_rows : (piece + 1) * w_rows, :]
+                if len(group) == 5:
+                    group[0][to % 2, to // 2] = got
+                else:
+                    group[0][to] = got
 
     for at in range(CTX):
         value_grads(at)
     qkv_pieces(s.gv, slice(2 * LANES, 3 * LANES))
-    grad_direct(s.gv, sem.gv)
+    grad_pair(s.gv, sem.gv)
     query_row(3)
-    grad_even_second(s.gi, sem.gi)
+    grad_steps(s.gi, sem.gi, half // 2, half)
     links.wait(s.go_side, sem.go_side, ctx_dev(opp))
-    s.go[0][...] = (s.go_two[side].astype(F32) + s.go_side[...].astype(F32)).astype(BF16)
-    grad_direct(s.go, sem.go)
+    for at in range(n_f):
+        s.go[0][at % 2, at // 2] = (
+            s.go_two[side, at].astype(F32) + s.go_side[at].astype(F32)
+        ).astype(BF16)
+    grad_pair(s.go, sem.go)
     query_row(2)
     pack(diag)
     pack(opp)
@@ -719,13 +725,15 @@
     sums = back_first(opp)
     scatter_second(s.rs_f, sem.rs_f, s.dsec[...])
     row_loop(sums)
+    grad_steps(s.gv, sem.gv)
     query_row(1)
+    grad_steps(s.go, sem.go)
     query_row(0)
     pack(sib)
     pack(c)
     qkv_pieces(s.gq, slice(0, 2 * LANES))
     grad_direct(s.gq, sem.gq)
-    grad_direct_sum(s.gv, sem.gv)
+    grad_even_third(s.gv, sem.gv)
     sums = back_first(sib)
     scatter_third(s.rs_f, sem.rs_f, s.dsec[...])
     row_loop(sums)
@@ -784,7 +792,7 @@
         total += s.vgf[lax.rem(f + step, n_f)]
     s.vgc[c] = total
     to_group(s.vgc, sem.vgc)
-    grad_direct_sum(s.go, sem.go)
+    grad_even_third(s.go, sem.go)
     grad_even_third(s.gi, sem.gi)
 
     scatter_wait(s.rs_o, sem.rs_o)
@@ -794,14 +802,14 @@
     keep(s.out, out_ref)
     from_group(s.gd[4], sem.gd[2])
     keep(s.gd[4], gdown_ref)
-    from_group(s.gv[2], sem.gv[1])
-    keep(s.gv[2], gv_ref)
+    from_group(s.gv[4], sem.gv[2])
+    keep(s.gv[4], gv_ref)
     from_group(s.gq[2], sem.gq[1])
     keep(s.gq[2], gqk_ref)
     from_group(s.vgc, sem.vgc)
     keep(s.vgc, small_ref)
-    from_group(s.go[2], sem.go[1])
-    keep(s.go[2], gout_ref)
+    from_group(s.go[4], sem.go[2])
+    keep(s.go[4], gout_ref)
     from_group(s.gi[4], sem.gi[2])
     keep(s.gi[4], gin_ref)
     links.drain()
@@ -923,7 +931,7 @@
         part = (z.half, size, cols)
         return [
             ((2,) + part, BF16),
-            (part, BF16, 1),
+            (part, BF16, z.half),
             (part, BF16),
             (part, BF16, 1),
             ((CTX, size, cols), BF16, 1),
@@ -998,10 +1006,10 @@
         rs_o=scatter(),
         rs_f=scatter(),
         gq=direct(z.w_rows, 2 * LANES),
-        gv=direct(z.w_rows, LANES),
+        gv=even(z.w_rows, LANES),
         gi=even(z.w_rows, z.own_ff),
         gd=even(z.part, width),
-        go=direct(out_part, width),
+        go=even(out_part, width),
         go_own=((2, 2) + out_rows, BF16),
         go_core=((2,) + out_rows, BF16, 1),
         go_two=((2,) + out_rows, BF16),
@@ -1094,7 +1102,7 @@
         out_specs=[far] * 8,
         scratch_shapes=[pltpu.VMEM(item[0], item[1]) for item in scratch_items(spec)]
         + [
-            pltpu.SemaphoreType.DMA((SENDS,)),
+            pltpu.SemaphoreType.DMA((SENDS if n_f == 8 else 8 * n_f,)),
             pltpu.SemaphoreType.DMA((n_recv,)),
             pltpu.SemaphoreType.DMA((26,)),
         ],

time: 88.7 us -> 83.3 us (0.939)
  the two profiles are of different devices: /device:TPU:27 before, /device:TPU:0 now
where the time goes in v3:
time: 83.3 us; the launch traced here: 83 us
  Pallas kernels  82.1 us (99%)
    pallas_call x1, Pallas kernels, per_device(): pl.pallas_call(functools.partial(layer_kernel, sizes), out_shape=[shaped(...  78.4 us
    pallas_call x1, Pallas kernels, per_device(): pl.pallas_call(functools.partial(finish_kernel, sizes), out_shape=[shaped...  3.76 us

profile of v3, /device:TPU:0, one launch (start us, length us, event | category | flops | bytes accessed | tf_op | source)
XLA Modules:
  0.0 83.0 jit_solution(13322109852450470527)
XLA Ops:
  0.7 78.4 %layer.1 = (bf16[256,512]{1,0:T(8,128)(2,1)}, bf16[256,512]{1,0:T(8,128)(2,1)}, bf16[4,64,256]{2,1,0:T(8,128)(2,1)}, bf16[4,64,128]{2,1,0:T(8,128)(2,1)}, bf16[4...) custom-call(bf16[256,512]{1,0:T(8,128)(2,1)} %bitcast.19, ...), custom_call_target="tpu_custom_call" | custom-call | tf_op jit(solution)/shard_map/layer/pallas_call | solution.py:1089
  79.0 3.8 %finish.1 = (bf16[256,512]{1,0:T(8,128)(2,1)}, bf16[256,512]{1,0:T(8,128)(2,1)}, f32[64,1536]{1,0:T(8,128)}, f32[64,512]{1,0:T(8,128)}, f32[64,2048]{1,0:T(8,128...) custom-call(bf16[256,512]{1,0:T(8,128)(2,1)} %get-tuple-element.34.o, ...), custom_call_target="tpu_custom_call" | custom-call | tf_op jit(solution)/shard_map/finish/pallas_call | solution.py:1145

commit v4 on v3

--- a/solution.py
+++ b/solution.py
@@ -358,6 +358,8 @@
             s.q[h, chunk] = jnp.transpose(kept).astype(BF16)
 
     first_norm(c)
+    for to in (sib, opp):
+        links.send(s.dy.at[c], s.dy.at[c], sem.dy + c, ctx_dev(to))
     pass_on(s.wq, sem.wq)
     to_peers(own_out, sem.wo[0])
     spread(s.wi, sem.wi)
@@ -368,8 +370,6 @@
     links.send(s.tok.at[opp], s.tok.at[opp], sem.tok + opp, ctx_dev(sib))
     first_norm(opp)
 
-    for to in (sib, opp):
-        links.send(s.dy.at[c], s.dy.at[c], sem.dy + c, ctx_dev(to))
 
     def share_out(to, block):
         links.send(s.wo.at[block], s.wo.at[block], sem.wo[1] + block, ctx_dev(to))
@@ -518,14 +518,14 @@
     pass_att(theirs[2])
     feed(opp)
     pass_att(theirs[3])
-    feed(sib)
-    feed(c)
     settle(s.wd, sem.wd)
     links.wait(s.dy.at[diag], sem.dy + diag, ctx_dev(sib))
     scatter_first(s.rs_s, sem.rs_s, feed_back(diag))
     scatter_second(s.rs_s, sem.rs_s, feed_back(opp))
+    feed(sib)
     links.wait(s.dy.at[sib], sem.dy + sib, ctx_dev(sib))
     scatter_third(s.rs_s, sem.rs_s, feed_back(sib))
+    feed(c)
     s.dsec[...] = feed_back(c)
 
     def even_pieces(group, left, right, cols, size):
@@ -727,6 +727,7 @@
     row_loop(sums)
     grad_steps(s.gv, sem.gv)
     query_row(1)
+    grad_even_third(s.gd, sem.gd)
     grad_steps(s.go, sem.go)
     query_row(0)
     pack(sib)
@@ -774,7 +775,6 @@
     pairs = [(s.vgp.at[lax.rem(f + step, n_f)], s.vgf.at[f]) for step in range(1, n_f)]
     links.send_all(pairs, sem.vgf, peers, s.vgf.at[0 : n_f - 1])
 
-    grad_even_third(s.gd, sem.gd)
     scatter_wait(s.rs_f, sem.rs_f)
 
     def first_back(rng):
@@ -785,6 +785,7 @@
 
     row_loop(first_back)
     keep(s.dx, dx_ref)
+    grad_even_third(s.gi, sem.gi)
     grad_direct_sum(s.gq, sem.gq)
     from_peers(s.vgf, sem.vgf)
     total = s.vgp[f]
@@ -793,7 +794,6 @@
     s.vgc[c] = total
     to_group(s.vgc, sem.vgc)
     grad_even_third(s.go, sem.go)
-    grad_even_third(s.gi, sem.gi)
 
     scatter_wait(s.rs_o, sem.rs_o)
     s.out[...] = (
@@ -851,6 +851,14 @@
     gdown_low,
     out_low,
     dx_low,
+    small,
+    gg1,
+    gs1,
+    gg2,
+    gs2,
+    gbi,
+    gbd,
+    grel,
     sems,
 ):
     made = []
@@ -868,13 +876,20 @@
         start(gout_in, gout_low),
     ]
     loads += [start(out_in, out_low), start(dx_in, dx_low), start(gv_in, gv_low)]
+    loads.append(start(small_in, small))
     width, own_ff = sizes.width, sizes.own_ff
+    stores = []
+    loads[4].wait()
+    stores.append(start(out_low, out_ref))
+    loads[5].wait()
+    stores.append(start(dx_low, dx_ref))
     loads[0].wait()
+    part = sizes.part
     for at in range(CTX):
-        gdown[at * sizes.part : (at + 1) * sizes.part, :] = gdown_low[at].astype(F32)
-    stores = [start(gdown, gdown_ref)]
+        lines = slice(at * part, (at + 1) * part)
+        gdown[lines, :] = gdown_low[at].astype(F32)
+        stores.append(start(gdown.at[lines, :], gdown_ref.at[lines, :]))
     loads[1].wait()
-    part = sizes.part
     for index in range(sizes.n_f):
         lanes = slice(index * part, (index + 1) * part)
         joined = jnp.concatenate([gin_low[at, :, lanes].astype(F32) for at in range(CTX)], axis=1)
@@ -896,19 +911,27 @@
     for at in range(CTX):
         gout[at * out_part : (at + 1) * out_part, :] = gout_low[at].astype(F32)
     stores.append(start(gout, gout_ref))
-    loads[4].wait()
-    stores.append(start(out_low, out_ref))
-    loads[5].wait()
-    stores.append(start(dx_low, dx_ref))
-    total = jnp.sum(small_in[...], axis=0)
-    for at, ref in enumerate((gg1_ref, gs1_ref, gg2_ref, gs2_ref, gbd_ref)):
+    loads[7].wait()
+    total = jnp.sum(small[...], axis=0)
+    for at, ref in enumerate((gg1, gs1, gg2, gs2, gbd)):
         ref[...] = total[at : at + 1, 0 : sizes.w_rows]
-    size = gbi_ref.shape[1]
-    hidden = jnp.concatenate([small_in[at, 5:6, 0 : sizes.part] for at in range(CTX)], axis=1)
-    for at in range(gbi_ref.shape[0]):
-        gbi_ref[at : at + 1, :] = hidden[:, at * size : (at + 1) * size]
+    size = gbi.shape[1]
+    hidden = jnp.concatenate([small[at, 5:6, 0:part] for at in range(CTX)], axis=1)
+    for at in range(gbi.shape[0]):
+        gbi[at : at + 1, :] = hidden[:, at * size : (at + 1) * size]
     for at in range(CTX):
-        grel_ref[2 * at : 2 * at + 2, :] = small_in[at, 6:8, 0 : sizes.buckets]
+        grel[2 * at : 2 * at + 2, :] = small[at, 6:8, 0 : sizes.buckets]
+    small_pairs = (
+        (gg1, gg1_ref),
+        (gs1, gs1_ref),
+        (gg2, gg2_ref),
+        (gs2, gs2_ref),
+        (gbi, gbi_ref),
+        (gbd, gbd_ref),
+        (grel, grel_ref),
+    )
+    for src, dst in small_pairs:
+        stores.append(start(src, dst))
     for copy in stores:
         copy.wait()
 
@@ -1145,11 +1168,12 @@
     done = pl.pallas_call(
         functools.partial(finish_kernel, sizes),
         out_shape=[shaped(shape, kind) for shape, kind in outs],
-        in_specs=[far] * 7 + [vmem],
-        out_specs=[far] * 6 + [vmem] * 7,
+        in_specs=[far] * 8,
+        out_specs=[far] * 13,
         scratch_shapes=[pltpu.VMEM(shape, kind) for shape, kind in outs[2:6]]
-        + [pltpu.VMEM(item.shape, item.dtype) for item in made[2:7] + made[0:2]]
-        + [pltpu.SemaphoreType.DMA((14,))],
+        + [pltpu.VMEM(item.shape, item.dtype) for item in made[2:7] + made[0:2] + made[7:8]]
+        + [pltpu.VMEM(shape, kind) for shape, kind in outs[6:]]
+        + [pltpu.SemaphoreType.DMA((28,))],
         compiler_params=pltpu.CompilerParams(vmem_limit_bytes=60 * 1024 * 1024),
         name="finish",
     )(*made)

time: 83.3 us -> 81.3 us (0.976)
  Pallas kernels: 82.1 us -> 79.5 us
    pallas_call x1, Pallas kernels: 78.4 us -> 76.8 us  [per_device(): pl.pallas_call(functools.partial(layer_kernel, sizes), out_shape=[shaped(...]
    pallas_call x1, Pallas kernels: 3.76 us -> 2.74 us  [per_device(): pl.pallas_call(functools.partial(finish_kernel, sizes), out_shape=[shaped...]
where the time goes in v4:
time: 81.3 us; the launch traced here: 80.4 us
  Pallas kernels  79.5 us (98%)
  between operations  0.82 us (1%)
    pallas_call x1, Pallas kernels, per_device(): pl.pallas_call(functools.partial(layer_kernel, sizes), out_shape=[shaped(...  76.8 us
    pallas_call x1, Pallas kernels, per_device(): pl.pallas_call(functools.partial(finish_kernel, sizes), out_shape=[shaped...  2.74 us

profile of v4, /device:TPU:0, one launch (start us, length us, event | category | flops | bytes accessed | tf_op | source)
XLA Modules:
  0.0 80.4 jit_solution(16503676342086800473)
XLA Ops:
  0.7 76.8 %layer.1 = (bf16[256,512]{1,0:T(8,128)(2,1)}, bf16[256,512]{1,0:T(8,128)(2,1)}, bf16[4,64,256]{2,1,0:T(8,128)(2,1)}, bf16[4,64,128]{2,1,0:T(8,128)(2,1)}, bf16[4...) custom-call(bf16[256,512]{1,0:T(8,128)(2,1)} %bitcast.19, ...), custom_call_target="tpu_custom_call" | custom-call | tf_op jit(solution)/shard_map/layer/pallas_call | solution.py:1112
  77.5 2.7 %finish.1 = (bf16[256,512]{1,0:T(8,128)(2,1)}, bf16[256,512]{1,0:T(8,128)(2,1)}, f32[64,1536]{1,0:T(8,128)}, f32[64,512]{1,0:T(8,128)}, f32[64,2048]{1,0:T(8,128...) custom-call(bf16[256,512]{1,0:T(8,128)(2,1)} %get-tuple-element.34.o, ...), custom_call_target="tpu_custom_call" | custom-call | tf_op jit(solution)/shard_map/finish/pallas_call | solution.py:1168
